TPU v7x, 512 devices: a whole 4x8x8 slice. The times are simulated.
512 devices in a mesh: gx: 4 (over x), gy: 64 (over z, y), gz: 2 (over core).
Axes of the slice: x: 4, y: 8, z: 8, core: 2. Of those that a mesh axis runs over, the one named last changes fastest.
Arguments:
- positions: float32 [3, 524288], P(None, ('gx', 'gy', 'gz')), as said below
- polarizability: float32 [4, 2, 524288], P(None, None, ('gx', 'gy', 'gz')), may hold values from -0.5 to 1
- applied_field: float32 [4, 2, 3, 524288], P(None, None, None, ('gx', 'gy', 'gz')), may hold values from -6 to 6
- pair_codes: int32 [12288], P(('gx', 'gy', 'gz')), may hold values from 0 to 1151
- pair_counts: int32 [512], P(('gx', 'gy', 'gz')), may hold values from 3 to 24, as said below
Outputs:
- dipoles: float32 [4, 2, 3, 524288], P(None, None, None, ('gx', 'gy', 'gz'))
Inputs may be any that keep to these rules, and one draw needn't show every extreme that they name: `pair_codes`: each code is ((dx + 1) * 3 + (dy + 1)) * 2 * 8^2 + zt * 8^2 + target_block * 8 + source_block with dx, dy in -1..1, zt in 0..1 and blocks in 0..7; only the first pair_counts entries of a device's list are live. `pair_counts`: some device has 24 live entries in every draw. `positions`: x and y lie in [0, 4) within the owner's slab cell; z lies in [2 z_half, 2 z_half + 2) for the owner's depth half.
All inputs are finite; a program needn't handle non-finite values.
Results may differ from a plain program's by a relative error of at most 0.0003.
Values sent between devices are 32-bit elements; how exact they have to be, the bound alone decides.
No kernel may reach another device: no remote copies, remote signals or barrier semaphores. Data moves between devices by JAX's collectives and lax.ppermute only.
A program may use at most 64 MiB of HBM per device.

v0:
```python
import math

import jax
import jax.numpy as jnp
from jax import lax
from jax.sharding import PartitionSpec as P

BLOCK = 128
ITERS = 4


cell_width = 4.0
soften = 1.0
screen = 0.5
coupling = 0.8


def from_behind(value, axis, steps):
    count = lax.axis_size(axis)
    pairs = [(source, (source + steps) % count) for source in range(count)]
    return lax.ppermute(value, axis, pairs)


def padded(block, sides, width):
    for axis, dim in sides:
        count = lax.axis_size(axis)
        forward = [(i, i + 1) for i in range(count - 1)]
        forward.append((count - 1, 0))
        backward = [(target, source) for source, target in forward]
        low = lax.ppermute(
            lax.slice_in_dim(block, block.shape[dim] - width, None, axis=dim), axis, forward
        )
        high = lax.ppermute(lax.slice_in_dim(block, 0, width, axis=dim), axis, backward)
        block = jnp.concatenate([low, block, high], axis=dim)
    return block


def tensor_field(tgt_pos, src_pos, shift_x, shift_y, sources):
    disp_x = tgt_pos[0][:, None] - src_pos[0][None, :] + shift_x
    disp_y = tgt_pos[1][:, None] - src_pos[1][None, :] + shift_y
    disp_z = tgt_pos[2][:, None] - src_pos[2][None, :]
    dist_sq = disp_x * disp_x + disp_y * disp_y + disp_z * disp_z + soften * soften
    inv_dist = lax.rsqrt(dist_sq)
    distance = dist_sq * inv_dist
    screened = jax.scipy.special.erfc(screen * distance)
    gaussian = 2.0 * screen / math.sqrt(math.pi) * jnp.exp(-screen * screen * dist_sq)
    inv_sq = inv_dist * inv_dist
    b_term = screened * inv_sq * inv_dist + gaussian * inv_sq
    c_term = (
        3.0 * screened * inv_sq * inv_dist + gaussian * (2.0 * screen * screen + 3.0 * inv_sq)
    ) * inv_sq
    disp_vec = jnp.stack([disp_x, disp_y, disp_z])
    tensor = (
        c_term[None, :, None, :]
        * disp_vec[:, :, None, :]
        * jnp.transpose(disp_vec, (1, 0, 2))[None, :, :, :]
    )
    tensor = tensor - jnp.eye(3, dtype=tensor.dtype)[:, None, :, None] * b_term[None, :, None, :]
    block_len = tgt_pos.shape[1]
    matrix = tensor.reshape(3 * block_len, 3 * block_len)
    flat_src = sources.reshape(-1, 3 * block_len)
    result = lax.dot_general(
        flat_src,
        matrix,
        (((1,), (1,)), ((), ())),
        precision=lax.Precision.HIGHEST,
        preferred_element_type=jnp.float32,
    )
    return result.reshape(sources.shape)


def carry(lower_part, upper_part):
    from_above = from_behind(lower_part, "gy", -1)
    from_below = from_behind(upper_part, "gy", 1)
    return from_above + from_below


def depth_sum(partial_value):
    return lax.psum_scatter(partial_value, "gz", scatter_dimension=3, tiled=True)


def shards(positions, polarizability, applied_field, pair_codes, pair_counts):
    freqs = polarizability.shape[0]
    local_rows = positions.shape[1]
    nblocks = local_rows // BLOCK
    square = nblocks * nblocks
    z_index = lax.axis_index("gz")
    pos_cube = positions.reshape(3, 1, 1, 1, local_rows)
    beside_all = padded(pos_cube, (("gx", 1), ("gy", 2), ("gz", 3)), 1)
    beside_all = beside_all.reshape(3, 27 * local_rows)
    a_re = polarizability[:, 0][:, None]
    a_im = polarizability[:, 1][:, None]

    def respond(field_re, field_im):
        return jnp.stack(
            [a_re * field_re - a_im * field_im, a_re * field_im + a_im * field_re], axis=1
        )

    def add_pair(partial_value, pair_code, sources, depth_src):
        src_block = pair_code % nblocks
        tgt_block = pair_code // nblocks % nblocks
        depth_tgt = pair_code // square % 2
        step_y = pair_code // (2 * square) % 3
        step_x = pair_code // (6 * square)
        src_start = (
            (step_x * 3 + 1) * 3 + depth_src - z_index + 1
        ) * local_rows + src_block * BLOCK
        tgt_start = ((3 + step_y) * 3 + depth_tgt - z_index + 1) * local_rows + tgt_block * BLOCK
        src_pos = lax.dynamic_slice_in_dim(beside_all, src_start, BLOCK, 1)
        tgt_pos = lax.dynamic_slice_in_dim(beside_all, tgt_start, BLOCK, 1)
        src_dip = lax.dynamic_slice_in_dim(
            sources, step_x * local_rows + src_block * BLOCK, BLOCK, 3
        )
        shift_x = (step_x - 1).astype(jnp.float32) * -cell_width
        shift_y = (step_y - 1).astype(jnp.float32) * cell_width
        contrib = tensor_field(tgt_pos, src_pos, shift_x, shift_y, src_dip)
        out_start = ((depth_tgt * 3 + step_y) * nblocks + tgt_block) * BLOCK
        previous = lax.dynamic_slice_in_dim(partial_value, out_start, BLOCK, 3)
        return lax.dynamic_update_slice_in_dim(partial_value, previous + contrib, out_start, 3)

    dipoles = respond(applied_field[:, 0], applied_field[:, 1])
    for sweep in range(ITERS):
        sources = padded(dipoles, (("gx", 3),), local_rows)
        partial_value = jnp.zeros((freqs, 2, 3, 6 * local_rows), jnp.float32)

        def own_entry(entry, partial_value):
            return add_pair(partial_value, pair_codes[entry], sources, z_index)

        partial_value = lax.fori_loop(0, pair_counts[0], own_entry, partial_value)
        partial_value = partial_value.reshape(freqs, 2, 3, 2, 3, local_rows)
        summed = depth_sum(partial_value)[:, :, :, 0]
        field = summed[:, :, :, 1] + carry(summed[:, :, :, 0], summed[:, :, :, 2])
        dipoles = respond(
            applied_field[:, 0] + coupling * field[:, 0],
            applied_field[:, 1] + coupling * field[:, 1],
        )
    return dipoles


def solution(mesh):
    in_specs = (
        P(None, ("gx", "gy", "gz")),
        P(None, None, ("gx", "gy", "gz")),
        P(None, None, None, ("gx", "gy", "gz")),
        P(("gx", "gy", "gz")),
        P(("gx", "gy", "gz")),
    )
    out_specs = P(None, None, None, ("gx", "gy", "gz"))
    return jax.shard_map(shards, mesh=mesh, in_specs=in_specs, out_specs=out_specs, check_vma=False)
```

profile of v0, /device:TPU:1, one launch (start us, length us, event | category | flops | bytes accessed | tf_op | source)
XLA Modules:
  0.0 913.5 jit_solution(6118828596474415320)
XLA Ops:
  6.5 3.9 collective-permute-start.2
  16.4 3.4 collective-permute-start.4
  19.8 12.3 %collective-permute-start.5 = (f32[3,3,1,1,1024]{4,0,3,2,1:T(4,128)S(1)}, f32[3,3,1,1,1024]{4,0,3,2,1:T(4,128)S(1)}, u32[]{:S(2)}, u32[]{:S(2)}) collective-permute-start(f32[3,3,1,1,1024]{4,0,3,2,1:T(4,128)S(1)} %pad_maximum_fusion.15), channel_id=1, source_target_pairs={{2,0},{4,2},{6,4},{8,6},{10,8},{12,10},{14,12},{16,14},{18,16},{20... | collective-permute-start | bytes 110600 | tf_op jit(solution)/shard_map/ppermute | solution.py:33
  34.0 4.6 collective-permute-start.1
  38.7 4.0 collective-permute-start.6
  46.7 47.0 %while.52 = (s32[]{:T(128)}, f32[4,2,3,6144]{3,0,2,1:T(4,128)S(1)}, s32[]{:T(128)}, s32[24]{0:T(128)S(1)}, f32[4,2,3,3072]{3,0,2,1:T(4,128)S(1)}, /*index=5*/s32...) while((s32[]{:T(128)}, f32[4,2,3,6144]{3,0,2,1:T(4,128)S(1)}, ...), condition=%wide.region_1.2_spmd, body=%wide.region_0.1_spmd.sunk | while | flops 16272520 | bytes 1500673 | solution.py:129
  95.8 141.7 %all-reduce.9.cloned.1.call-done = f32[4,2,3,2,3,1024]{5,0,4,3,2,1:T(4,128)} async-done(((f32[4,2,3,2,3,1024]{5,0,4,3,2,1:T(4,128)}), f32[4,2,3,2,3,1024]{5,0,4,3,2,1:T(4,128)}) %all-reduce.9.cloned.1.call-update) | async-done | bytes 589840
  239.1 6.9 collective-permute-start.8
  247.9 7.1 collective-permute-done.9
  258.3 3.4 collective-permute-start.11
  264.0 47.0 %while.53 = (s32[]{:T(128)}, f32[4,2,3,6144]{3,0,2,1:T(4,128)S(1)}, s32[]{:T(128)}, s32[24]{0:T(128)S(1)}, f32[4,2,3,3072]{3,0,2,1:T(4,128)S(1)}, /*index=5*/s32...) while((s32[]{:T(128)}, f32[4,2,3,6144]{3,0,2,1:T(4,128)S(1)}, ...), condition=%wide.region_4.5_spmd, body=%wide.region_3.4_spmd.sunk | while | flops 16272520 | bytes 1500673 | solution.py:129
  311.9 142.6 %all-reduce.11.cloned.1.call-done = f32[4,2,3,2,3,1024]{5,0,2,1,4,3:T(4,128)} async-done(((f32[4,2,3,2,3,1024]{5,0,2,1,4,3:T(4,128)}), f32[4,2,3,2,3,1024]{5,0,2,1,4,3:T(4,128)}) %all-reduce.11.cloned.1.call-update) | async-done | bytes 589840
  456.1 6.9 collective-permute-start.12
  464.9 7.1 collective-permute-done.13
  475.3 3.4 collective-permute-start.15
  481.0 47.0 %while.54 = (s32[]{:T(128)}, f32[4,2,3,6144]{3,0,2,1:T(4,128)S(1)}, s32[]{:T(128)}, s32[24]{0:T(128)S(1)}, f32[4,2,3,3072]{3,0,2,1:T(4,128)S(1)}, /*index=5*/s32...) while((s32[]{:T(128)}, f32[4,2,3,6144]{3,0,2,1:T(4,128)S(1)}, ...), condition=%wide.region_7.8_spmd, body=%wide.region_6.7_spmd.sunk | while | flops 16272520 | bytes 1500673 | solution.py:129
  528.9 142.6 %all-reduce.13.cloned.1.call-done = f32[4,2,3,2,3,1024]{5,0,2,1,4,3:T(4,128)} async-done(((f32[4,2,3,2,3,1024]{5,0,2,1,4,3:T(4,128)}), f32[4,2,3,2,3,1024]{5,0,2,1,4,3:T(4,128)}) %all-reduce.13.cloned.1.call-update) | async-done | bytes 589840
  673.1 6.9 collective-permute-start.16
  681.9 7.1 collective-permute-done.17
  692.3 3.4 collective-permute-start.19
  698.0 47.0 %while.55 = (s32[]{:T(128)}, f32[4,2,3,6144]{3,0,2,1:T(4,128)S(1)}, s32[]{:T(128)}, s32[24]{0:T(128)S(1)}, f32[4,2,3,3072]{3,0,2,1:T(4,128)S(1)}, /*index=5*/s32...) while((s32[]{:T(128)}, f32[4,2,3,6144]{3,0,2,1:T(4,128)S(1)}, ...), condition=%wide.region_10.11_spmd, body=%wide.region_9.10_spmd.sunk | while | flops 16272520 | bytes 1500673 | solution.py:129
  745.9 142.7 %all-reduce.15.cloned.1.call-done = f32[4,2,3,2,3,1024]{5,0,2,1,4,3:T(4,128)} async-done(((f32[4,2,3,2,3,1024]{5,0,2,1,4,3:T(4,128)}), f32[4,2,3,2,3,1024]{5,0,2,1,4,3:T(4,128)}) %all-reduce.15.cloned.1.call-update) | async-done | bytes 589840
  890.2 6.9 collective-permute-start.20
  899.0 7.1 collective-permute-done.21
  (363 shorter events, 103.5 us)
Async XLA Ops:
  6.5 231.0 %all-reduce.9.cloned.1.call-start = ((), (), s32[]{:S(2)}) async-start(), calls=%async_computation | async-start | bytes 1179648
  6.5 9.1 %collective-permute-start.2 = (f32[3,1,1,1,1024]{4,0,3,2,1:T(4,128)}, f32[3,1,1,1,1024]{4,0,3,2,1:T(4,128)S(1)}, u32[]{:S(2)}, u32[]{:S(2)}) collective-permute-start(f32[3,1,1,1,1024]{4,0,3,2,1:T(4,128)} %bitcast.225), channel_id=1, source_target_pairs={{0,128},{128,256},{256,384},{384,0},{1,129},{129,257},{257,385},{3... | collective-permute-start | bytes 36872 | tf_op jit(solution)/shard_map/ppermute | solution.py:30
  16.4 22.2 %collective-permute-start.4 = (f32[3,3,1,1,1024]{4,0,3,2,1:T(4,128)S(1)}, f32[3,3,1,1,1024]{4,0,3,2,1:T(4,128)S(1)}, u32[]{:S(2)}, u32[]{:S(2)}) collective-permute-start(f32[3,3,1,1,1024]{4,0,3,2,1:T(4,128)S(1)} %pad_maximum_fusion.15), channel_id=1, source_target_pairs={{0,2},{2,4},{4,6},{6,8},{8,10},{10,12},{12,14},{14,16},{16,18},{18... | collective-permute-start | bytes 110600 | tf_op jit(solution)/shard_map/ppermute | solution.py:30
  19.8 18.9 %collective-permute-start.5 = (f32[3,3,1,1,1024]{4,0,3,2,1:T(4,128)S(1)}, f32[3,3,1,1,1024]{4,0,3,2,1:T(4,128)S(1)}, u32[]{:S(2)}, u32[]{:S(2)}) collective-permute-start(f32[3,3,1,1,1024]{4,0,3,2,1:T(4,128)S(1)} %pad_maximum_fusion.15), channel_id=1, source_target_pairs={{2,0},{4,2},{6,4},{8,6},{10,8},{12,10},{14,12},{16,14},{18,16},{20... | collective-permute-start | bytes 110600 | tf_op jit(solution)/shard_map/ppermute | solution.py:33
  32.1 12.5 %collective-permute-start = (f32[4,2,3,1024]{3,0,2,1:T(4,128)S(1)}, f32[4,2,3,1024]{3,0,2,1:T(4,128)S(1)}, u32[]{:S(2)}, u32[]{:S(2)}) collective-permute-start(f32[4,2,3,1024]{3,0,2,1:T(4,128)S(1)} %pad_maximum_fusion.10), channel_id=1, source_target_pairs={{0,128},{128,256},{256,384},{384,0},{1,129},{129,257},{257,385},{3... | collective-permute-start | bytes 294920 | tf_op jit(solution)/shard_map/ppermute | solution.py:30
  34.0 10.6 %collective-permute-start.1 = (f32[4,2,3,1024]{3,0,2,1:T(4,128)S(1)}, f32[4,2,3,1024]{3,0,2,1:T(4,128)S(1)}, u32[]{:S(2)}, u32[]{:S(2)}) collective-permute-start(f32[4,2,3,1024]{3,0,2,1:T(4,128)S(1)} %pad_maximum_fusion.10), channel_id=1, source_target_pairs={{128,0},{256,128},{384,256},{0,384},{129,1},{257,129},{385,257},{1... | collective-permute-start | bytes 294920 | tf_op jit(solution)/shard_map/ppermute | solution.py:33
  38.7 6.0 collective-permute-start.6
  94.5 360.0 %all-reduce.11.cloned.1.call-start = ((), (), s32[]{:S(2)}) async-start(), calls=%async_computation.1 | async-start | bytes 1179648
  239.1 8.8 collective-permute-start.8
  245.9 9.1 collective-permute-start.9
  255.2 6.6 collective-permute-start.10
  258.3 5.6 collective-permute-start.11
  311.9 359.7 %all-reduce.13.cloned.1.call-start = ((), (), s32[]{:S(2)}) async-start(), calls=%async_computation.2 | async-start | bytes 1179648
  456.1 8.8 collective-permute-start.12
  463.0 9.1 collective-permute-start.13
  472.2 6.6 collective-permute-start.14
  475.3 5.6 collective-permute-start.15
  528.9 359.7 %all-reduce.15.cloned.1.call-start = ((), (), s32[]{:S(2)}) async-start(), calls=%async_computation.3 | async-start | bytes 1179648
  673.1 8.8 collective-permute-start.16
  680.0 9.1 collective-permute-start.17
  689.2 6.6 collective-permute-start.18
  692.3 5.6 collective-permute-start.19
  890.2 8.8 collective-permute-start.20
  897.0 9.1 collective-permute-start.21
  (5 other events, 10.7 us)
Sparse Core Ops, SparseCore 0:
  94.7 142.8 all-reduce.8
  312.0 142.5 all-reduce.10
  529.0 142.5 all-reduce.12
  746.0 142.5 all-reduce.14
where the time goes:
time: 920 us; the launch traced here: 913 us
  waiting for transfers between devices  606 us (66%)
  loops' own time  132 us (14%)
  starting transfers between devices  89.9 us (10%)
  local copies, waits for them, and re-layouts  33.6 us (4%)
  matrix products  20.7 us (2%)
  other arithmetic  17.2 us (2%)
  between operations  13.6 us (1%)
    unnamed x8, waiting for transfers between devices  570 us
    another operation x4, loops' own time, shards(): partial_value = lax.fori_loop(0, pair_counts[0], own_entry, partial_value)  132 us
    ppermute x8, starting transfers between devices, from_behind(): return lax.ppermute(value, axis, pairs)  35.1 us
    ppermute x7, starting transfers between devices, padded(): lax.ppermute(lax.slice_in_dim(block, 0, width, axis=dim), axis, backward)  32.2 us
    ppermute x8, waiting for transfers between devices, from_behind(): return lax.ppermute(value, axis, pairs)  28.6 us
    ppermute x7, starting transfers between devices, padded(): lax.ppermute(lax.slice_in_dim(block, block.shape[dim] - width, None, axis...  22.5 us
    dot_general x28, matrix products, tensor_field(): lax.dot_general(flat_src, matrix, (((1,), (1,)), ((), ())), precision=lax...  20.7 us
  transfers between devices with their start and end apart: 26, of which 15 were waited for; matrix products, arithmetic and copies ran while one was open for 0% of the time, Pallas kernels for 0%

commit v1 on v0

v1 whole, which is shorter than its diff:
```python
import functools
import math

import jax
import jax.numpy as jnp
from jax import lax
from jax.experimental import pallas as pl
from jax.experimental.pallas import tpu as pltpu
from jax.sharding import PartitionSpec as P

BLOCK = 128
ITERS = 4

cell_width = 4.0
coupling = 0.8
root_pi = 1.0 / math.sqrt(math.pi)
erfcx_fit = (
    1.790011536,
    0.928601473,
    0.3238769782,
    0.05183749415,
    -0.01103335474,
    -0.006028563159,
    0.0006207049413,
    0.0006951546236,
    -6.044884693e-05,
    -6.930253734e-05,
)

VMEM = pl.BlockSpec(memory_space=pltpu.VMEM)
SMEM = pl.BlockSpec(memory_space=pltpu.SMEM)


def swaps(count, first):
    if first:
        return [(i, i ^ 1) for i in range(count)]
    return [(i, (i + 1) % count if i % 2 else (i - 1) % count) for i in range(count)]


def exchange(value, axis):
    count = lax.axis_size(axis)
    return (
        lax.ppermute(value, axis, swaps(count, True)),
        lax.ppermute(value, axis, swaps(count, False)),
    )


def rows_of(value, block):
    return value[:, pl.ds(pl.multiple_of(block * BLOCK, BLOCK), BLOCK)]


def lower_half(shape):
    return lax.broadcasted_iota(jnp.int32, shape, 0) % 8 < 4


def build(word, src_slot, spos, tpos, tens):
    entry = word & 63
    src_block = (word >> 6) & 7
    half = (word >> 9) & 1
    tgt_block = (word >> 10) & 7
    tgt_half = (word >> 13) & 1
    tgt_slot = (word >> 14) & 3
    shift_x = (((word >> 16) & 3) - 1).astype(jnp.float32) * -cell_width
    shift_y = (((word >> 18) & 3) - 1).astype(jnp.float32) * cell_width
    src = spos.at[src_slot * 2 + half]
    src_cols = pl.ds(pl.multiple_of(src_block * BLOCK, BLOCK), BLOCK)
    tgt_cols = pl.ds(pl.multiple_of(tgt_block * BLOCK, BLOCK), BLOCK)
    sx, sy, sz = (src[k : k + 1, src_cols] for k in range(3))
    tgt = jnp.transpose(tpos[tgt_slot * 2 + tgt_half, :, tgt_cols])
    chunk = 32
    for start in range(0, BLOCK, chunk):
        part = tgt[start : start + chunk]
        dx = part[:, 0:1] - sx + shift_x
        dy = part[:, 1:2] - sy + shift_y
        dz = part[:, 2:3] - sz
        dist_sq = dx * dx + dy * dy + dz * dz + 1.0
        inv_dist = lax.rsqrt(dist_sq)
        distance = dist_sq * inv_dist
        inv_sq = inv_dist * inv_dist
        reach = 1.0 / (distance + 4.0)
        at = reach * 10.0 - 1.0
        fit = jnp.full_like(at, erfcx_fit[-1])
        for coef in erfcx_fit[-2::-1]:
            fit = fit * at + coef
        decay = jnp.exp(dist_sq * -0.25)
        b_term = inv_sq * decay * (fit * reach * inv_dist + root_pi)
        c_term = inv_sq * (3.0 * b_term + (0.5 * root_pi) * decay)
        cx, cy, cz = c_term * dx, c_term * dy, c_term * dz
        comps = (cx * dx - b_term, cx * dy, cx * dz, cy * dy - b_term, cy * dz, cz * dz - b_term)
        for k, comp in enumerate(comps):
            high = comp.astype(jnp.bfloat16)
            low = (comp - high.astype(jnp.float32)).astype(jnp.bfloat16)
            tens[entry, pl.ds(k * BLOCK + start, chunk), 0:BLOCK] = high
            tens[entry, pl.ds(k * BLOCK + start, chunk), BLOCK : 2 * BLOCK] = low


def apply(word, dip, tens, out, self_target):
    entry = word & 63
    src_block = (word >> 6) & 7
    half = (word >> 9) & 1
    tgt_block = (word >> 10) & 7
    tgt_half = (word >> 13) & 1
    tgt_slot = (word >> 14) & 3
    cols = pl.ds(pl.multiple_of(src_block * BLOCK, BLOCK), BLOCK)
    value = dip[0:24, cols]
    mine = (lax.broadcasted_iota(jnp.int32, (24, BLOCK), 0) % 8 // 4) == half
    high = value.astype(jnp.bfloat16).astype(jnp.float32)
    low = value - high
    low = jnp.concatenate([pltpu.roll(low[8 * k : 8 * k + 8], 4, 0) for k in range(3)], axis=0)
    left = jnp.where(mine, high, low)
    right = jnp.where(mine, high, 0.0)
    lhs = jnp.concatenate([left, right], axis=1).astype(jnp.bfloat16)
    res = lax.dot_general(
        lhs, tens[entry], (((1,), (1,)), ((), ())), preferred_element_type=jnp.float32
    )
    pick = ((0, 1, 2), (1, 3, 4), (2, 4, 5))
    outcols = pl.ds(pl.multiple_of(tgt_block * BLOCK, BLOCK), BLOCK)
    place = tgt_half if self_target else (tgt_slot - 1) * 2 + tgt_half
    for a in range(3):
        total = out[place, 8 * a : 8 * a + 8, outcols]
        for b in range(3):
            k = pick[a][b]
            total = total + res[8 * b : 8 * b + 8, k * BLOCK : (k + 1) * BLOCK]
        out[place, 8 * a : 8 * a + 8, outcols] = total


def each(tab, group, body):
    base = group * 64

    def step(i, carry):
        body(tab[base + 1 + i])
        return carry

    lax.fori_loop(0, tab[base], step, 0)


def settle(acc, place, out, out_row=0):
    for a in range(3):
        own, other = acc[place, 8 * a : 8 * a + 8, :], acc[place + 1, 8 * a : 8 * a + 8, :]
        own = own + pltpu.roll(own, 4, 0)
        other = other + pltpu.roll(other, 4, 0)
        out[8 * a : 8 * a + 8, :] = jnp.where(lower_half(own.shape), own, other)


def first_kernel(lists, own, xa, xb, ya, yb, tens, tab, msg_a, msg_b, spos, tpos, acc):
    for group in range(6):
        tab[group * 64] = 0
    core, even_x, even_y = lists[50], lists[51], lists[52]
    for half in range(2):

        def place(p, carry, half=half):
            code = lists[half * 25 + p]
            steps = code >> 7
            step_x = (steps * 11) >> 5
            step_y = steps - 3 * step_x
            slot_x = jnp.where(step_x == 1, 0, jnp.where((step_x == 2) == (even_x == 1), 1, 2))
            slot_y = jnp.where(step_y == 1, 0, jnp.where((step_y == 2) == (even_y == 1), 1, 2))
            tgt_half = ((code >> 6) & 1) ^ core
            word = (
                (half * 24 + p)
                | ((code & 7) << 6)
                | (half << 9)
                | (((code >> 3) & 7) << 10)
                | (tgt_half << 13)
                | (slot_y << 14)
                | (step_x << 16)
                | (step_y << 18)
            )
            group = slot_x + jnp.where(slot_y == 0, 3, 0)
            at = tab[group * 64]
            tab[group * 64 + 1 + at] = word
            tab[group * 64] = at + 1
            return carry

        lax.fori_loop(0, lists[half * 25 + 24], place, 0)
    for slot, (source, target) in enumerate(((own, own), (xa, ya), (xb, yb))):
        base = 24
        for half in range(2):
            spos[slot * 2 + half, 0:3, :] = source[base + 3 * half : base + 3 * half + 3, :]
            row = base if slot == 0 else 0
            tpos[slot * 2 + half, 0:3, :] = target[row + 3 * half : row + 3 * half + 3, :]
    acc[...] = jnp.zeros_like(acc)
    for slot, dip in enumerate((own, xa, xb)):

        def both(word, slot=slot, dip=dip):
            build(word, slot, spos, tpos, tens)
            apply(word, dip, tens, acc, False)

        each(tab, slot, both)
    settle(acc, 0, msg_a)
    settle(acc, 2, msg_b)


def second_kernel(tab, own, xa, xb, tens_in, field, tens, spos, acc):
    for slot, source in enumerate((own, xa, xb)):
        for half in range(2):
            spos[slot * 2 + half, 0:3, :] = source[24 + 3 * half : 27 + 3 * half, :]
    acc[...] = jnp.zeros_like(acc)
    for slot, dip in enumerate((own, xa, xb)):

        def both(word, slot=slot, dip=dip):
            build(word, slot, spos, spos, tens)
            apply(word, dip, tens, acc, True)

        each(tab, slot + 3, both)
    settle(acc, 0, field)


def local_kernel(tab, own, tens, acc_far, acc_near):
    acc_far[...] = jnp.zeros_like(acc_far)
    acc_near[...] = jnp.zeros_like(acc_near)
    each(tab, 0, lambda word: apply(word, own, tens, acc_far, False))
    each(tab, 3, lambda word: apply(word, own, tens, acc_near, True))


def far_kernel(tab, xa, xb, tens, acc_in, msg_a, msg_b, acc):
    acc[...] = acc_in[...]
    each(tab, 1, lambda word: apply(word, xa, tens, acc, False))
    each(tab, 2, lambda word: apply(word, xb, tens, acc, False))
    settle(acc, 0, msg_a)
    settle(acc, 2, msg_b)


def near_kernel(tab, xa, xb, tens, acc_in, field, acc):
    acc[...] = acc_in[...]
    each(tab, 4, lambda word: apply(word, xa, tens, acc, True))
    each(tab, 5, lambda word: apply(word, xb, tens, acc, True))
    settle(acc, 0, field)


def respond_rows(alpha, total):
    real_row = lax.broadcasted_iota(jnp.int32, (8, total.shape[1]), 0) % 4 < 2
    turned = jnp.where(real_row, pltpu.roll(total, 6, 0), pltpu.roll(total, 2, 0))
    return alpha[0:8] * total + alpha[8:16] * turned


def update_kernel(field, from_a, from_b, applied, alpha, dip):
    for a in range(3):
        rows = slice(8 * a, 8 * a + 8)
        total = applied[rows, :] + coupling * (field[rows, :] + from_a[rows, :] + from_b[rows, :])
        dip[rows, :] = respond_rows(alpha[...], total)


def start_kernel(applied, alpha, pos, dip):
    for a in range(3):
        rows = slice(8 * a, 8 * a + 8)
        dip[rows, :] = respond_rows(alpha[...], applied[rows, :])
    dip[24:32, :] = pos[...]


def call(body, out_shape, scratch=(), in_specs=None, out_specs=None, aliases=None):
    specs = {} if in_specs is None else {"in_specs": in_specs, "out_specs": out_specs}
    return pl.pallas_call(
        body,
        out_shape=out_shape,
        **specs,
        scratch_shapes=list(scratch),
        input_output_aliases=aliases or {},
        compiler_params=pltpu.CompilerParams(vmem_limit_bytes=16 * 1024 * 1024),
    )


def shards(positions, polarizability, applied_field, pair_codes, pair_counts):
    rows = positions.shape[1]
    entries = pair_codes.shape[0]
    half_freqs = polarizability.shape[0] // 2
    core = lax.axis_index("gz")
    f32 = jnp.float32
    arr = lambda r: jax.ShapeDtypeStruct((r, rows), f32)
    pack = lambda f, a: jnp.concatenate(
        [
            jnp.transpose(f, (2, 1, 0, 3)).reshape(12, rows),
            jnp.transpose(a, (1, 0, 2)).reshape(4, rows),
        ],
        axis=0,
    )
    freqs_of = lambda v, c: lax.dynamic_slice_in_dim(v, c * half_freqs, half_freqs, 0)
    mine = pack(freqs_of(applied_field, core), freqs_of(polarizability, core))
    theirs = pack(freqs_of(applied_field, 1 - core), freqs_of(polarizability, 1 - core))
    codes = jnp.concatenate([pair_codes, pair_counts])
    codes_row = jnp.pad(codes.astype(f32), (0, rows - entries - 1))[None]
    sent = jnp.concatenate([theirs, positions, codes_row], axis=0)
    got = lax.ppermute(sent, "gz", swaps(2, True))
    join = lambda u, v, k: jnp.stack([u.reshape(k, 4, rows), v.reshape(k, 4, rows)], axis=1).reshape(8 * k, rows)
    applied = join(mine[:12], got[:12], 3)
    base = join(mine[12:16], got[12:16], 1).reshape(2, 2, 2, rows)
    real = jnp.broadcast_to(base[:, :1], base.shape).reshape(8, rows)
    imag = base[:, 1:]
    imag = jnp.concatenate([-imag, imag], axis=1).reshape(8, rows)
    alpha = jnp.concatenate([real, imag], axis=0)
    pos = jnp.concatenate([positions, got[16:19], jnp.zeros((2, rows), f32)], axis=0)
    parity = lambda axis: 1 - lax.axis_index(axis) % 2
    lists = jnp.concatenate(
        [
            codes,
            got[19, : entries + 1].astype(jnp.int32),
            jnp.stack([core, parity("gx"), parity("gy")]).astype(jnp.int32),
        ]
    )
    ya, yb = exchange(pos, "gy")
    own = call(start_kernel, arr(32))(applied, alpha, pos)
    xa, xb = exchange(own, "gx")
    tens_shape = pltpu.VMEM((2 * entries, 6 * BLOCK, 2 * BLOCK), jnp.bfloat16)
    keep = lambda v: pltpu.with_memory_space_constraint(v, pltpu.VMEM)
    tab_shape = jax.ShapeDtypeStruct((6 * 64,), jnp.int32)
    far_shape = jax.ShapeDtypeStruct((4, 24, rows), f32)
    near_shape = jax.ShapeDtypeStruct((2, 24, rows), f32)
    far_scratch = pltpu.VMEM((4, 24, rows), f32)
    near_scratch = pltpu.VMEM((2, 24, rows), f32)
    pos_scratch = pltpu.VMEM((6, 8, rows), f32)
    tens, tab, msg_a, msg_b = call(
        first_kernel,
        (tens_shape, tab_shape, arr(24), arr(24)),
        (pos_scratch, pos_scratch, far_scratch),
        [SMEM] + [VMEM] * 5,
        (VMEM, SMEM, VMEM, VMEM),
    )(lists, own, xa, xb, ya, yb)
    from_a, from_b = swap_back(msg_a, msg_b)
    field, tens = call(
        second_kernel,
        (arr(24), tens_shape),
        (pos_scratch, near_scratch),
        [SMEM] + [VMEM] * 4,
        (VMEM, VMEM),
        {4: 1},
    )(tab, own, xa, xb, keep(tens))
    dip = call(update_kernel, arr(24))(field, from_a, from_b, applied, alpha)
    for sweep in range(1, ITERS):
        xa, xb = exchange(dip, "gx")
        far, near = call(
            local_kernel, (far_shape, near_shape), (), [SMEM] + [VMEM] * 2, (VMEM, VMEM)
        )(tab, dip, keep(tens))
        msg_a, msg_b = call(
            far_kernel, (arr(24), arr(24)), (far_scratch,), [SMEM] + [VMEM] * 4, (VMEM, VMEM)
        )(tab, xa, xb, keep(tens), far)
        from_a, from_b = swap_back(msg_a, msg_b)
        field = call(near_kernel, arr(24), (near_scratch,), [SMEM] + [VMEM] * 4, VMEM)(
            tab, xa, xb, keep(tens), near
        )
        dip = call(update_kernel, arr(24))(field, from_a, from_b, applied, alpha)
    dip = dip.reshape(3, 2, 2, half_freqs, rows)
    kept = jnp.transpose(dip[:, 0], (2, 1, 0, 3))
    passed = lax.ppermute(jnp.transpose(dip[:, 1], (2, 1, 0, 3)), "gz", swaps(2, True))
    return jnp.where(
        core == 0, jnp.concatenate([kept, passed]), jnp.concatenate([passed, kept])
    )


def swap_back(msg_a, msg_b):
    count = lax.axis_size("gy")
    return (
        lax.ppermute(msg_a, "gy", swaps(count, True)),
        lax.ppermute(msg_b, "gy", swaps(count, False)),
    )


def solution(mesh):
    in_specs = (
        P(None, ("gx", "gy", "gz")),
        P(None, None, ("gx", "gy", "gz")),
        P(None, None, None, ("gx", "gy", "gz")),
        P(("gx", "gy", "gz")),
        P(("gx", "gy", "gz")),
    )
    out_specs = P(None, None, None, ("gx", "gy", "gz"))
    return jax.shard_map(shards, mesh=mesh, in_specs=in_specs, out_specs=out_specs, check_vma=False)
```

time: 920 us -> 157 us (0.17)
  the two profiles are of different devices: /device:TPU:1 before, /device:TPU:3 now
where the time goes in v1:
time: 157 us; the launch traced here: 156 us
  Pallas kernels  76.8 us (49%)
  starting transfers between devices  59.7 us (38%)
  waiting for transfers between devices  12.4 us (8%)
  other arithmetic  3.05 us (2%)
  local copies, waits for them, and re-layouts  2.9 us (2%)
    ppermute x5, starting transfers between devices, exchange(): lax.ppermute(value, axis, swaps(count, False))  22.4 us
    pallas_call x1, Pallas kernels, shards(): call(first_kernel, (tens_shape, tab_shape, arr(24), arr(24)), (pos_scratc...  22.2 us
    pallas_call x3, Pallas kernels, shards(): call(far_kernel, (arr(24), arr(24)), (far_scratch,), [SMEM] + [VMEM] * 4,...  18 us
    pallas_call x3, Pallas kernels, shards(): call(local_kernel, (far_shape, near_shape), (), [SMEM] + [VMEM] * 2, (VME...  14.4 us
    pallas_call x3, Pallas kernels, shards(): call(near_kernel, arr(24), (near_scratch,), [SMEM] + [VMEM] * 4, VMEM)  11.4 us
    ppermute x5, starting transfers between devices, exchange(): lax.ppermute(value, axis, swaps(count, True))  11.1 us
    pallas_call x1, Pallas kernels, shards(): call(second_kernel, (arr(24), tens_shape), (pos_scratch, near_scratch), [...  10.6 us
    ppermute x4, waiting for transfers between devices, swap_back(): lax.ppermute(msg_b, 'gy', swaps(count, False))  8.77 us
  transfers between devices with their start and end apart: 20, of which 9 were waited for; matrix products, arithmetic and copies ran while one was open for 1% of the time, Pallas kernels for 23%

profile of v1, /device:TPU:3, one launch (start us, length us, event | category | flops | bytes accessed | tf_op | source)
XLA Modules:
  0.0 156.2 jit_solution(9043497347763534845)
XLA Ops:
  3.8 2.6 %collective-permute-start = (f32[20,1024]{1,0:T(8,128)S(1)}, f32[20,1024]{1,0:T(8,128)S(1)}, u32[]{:S(2)}, u32[]{:S(2)}) collective-permute-start(f32[20,1024]{1,0:T(8,128)S(1)} %pad_maximum_fusion), channel_id=1, source_target_pairs={{0,1},{1,0},{2,3},{3,2},{4,5},{5,4},{6,7},{7,6},{8,9},{9,8},{10,11... | collective-permute-start | bytes 245768 | tf_op jit(solution)/shard_map/ppermute | solution.py:283
  8.1 13.6 %collective-permute-start.4 = (f32[8,1024]{1,0:T(8,128)S(1)}, f32[8,1024]{1,0:T(8,128)S(1)}, u32[]{:S(2)}, u32[]{:S(2)}) collective-permute-start(f32[8,1024]{1,0:T(8,128)S(1)} %maximum_maximum_fusion.pos), channel_id=1, source_target_pairs={{0,126},{2,4},{4,2},{6,8},{8,6},{10,12},{12,10},{14,16},{16,14},{1... | collective-permute-start | bytes 98312 | tf_op jit(solution)/shard_map/ppermute | solution.py:44
  24.1 3.1 %collective-permute-start.2 = (f32[32,1024]{1,0:T(8,128)S(1)}, f32[32,1024]{1,0:T(8,128)S(1)}, u32[]{:S(2)}, u32[]{:S(2)}) collective-permute-start(f32[32,1024]{1,0:T(8,128)S(1)} %shard_map.55.own), channel_id=1, source_target_pairs={{0,384},{128,256},{256,128},{384,0},{1,385},{129,257},{257,129},{3... | collective-permute-start | bytes 393224 | tf_op jit(solution)/shard_map/ppermute | solution.py:44
  27.2 3.4 %collective-permute-start.1 = (f32[32,1024]{1,0:T(8,128)S(1)}, f32[32,1024]{1,0:T(8,128)S(1)}, u32[]{:S(2)}, u32[]{:S(2)}) collective-permute-start(f32[32,1024]{1,0:T(8,128)S(1)} %shard_map.55.own), channel_id=1, source_target_pairs={{0,128},{128,0},{256,384},{384,256},{1,129},{129,1},{257,385},{385... | collective-permute-start | bytes 393224 | tf_op jit(solution)/shard_map/ppermute | solution.py:43
  31.4 1.9 %collective-permute-done.1.xa = f32[32,1024]{1,0:T(8,128)S(1)} collective-permute-done((f32[32,1024]{1,0:T(8,128)S(1)}, f32[32,1024]{1,0:T(8,128)S(1)}, u32[]{:S(2)}, u32[]{:S(2)}) %collective-permute-start.1) | collective-permute-done | bytes 131104 | tf_op jit(solution)/shard_map/ppermute | solution.py:43
  33.3 22.2 %shard_map.56 = (bf16[48,768,256]{2,1,0:T(8,128)(2,1)S(1)}, s32[384]{0:T(512)S(1)}, f32[24,1024]{1,0:T(8,128)S(1)}, f32[24,1024]{1,0:T(8,128)S(1)}) custom-call(s32[53]{0:T(128)S(1)} %concatenate.28.lists, f32[32,1024]{1,0:T(8,128)S(1)} %shard_map.55.own, f32[32,1024]{1,0:T(8,128)S(1)} %collective-permute-done.1.xa, ...), custom_call_target="tpu_custom_call" | custom-call | tf_op jit(solution)/shard_map/pallas_call | solution.py:311
  55.5 1.9 %collective-permute-start.5 = (f32[24,1024]{1,0:T(8,128)S(1)}, f32[24,1024]{1,0:T(8,128)S(1)}, u32[]{:S(2)}, u32[]{:S(2)}) collective-permute-start(f32[24,1024]{1,0:T(8,128)S(1)} %get-tuple-element.26), channel_id=1, source_target_pairs={{0,2},{2,0},{4,6},{6,4},{8,10},{10,8},{12,14},{14,12},{16,18},{18,... | collective-permute-start | bytes 294920 | tf_op jit(solution)/shard_map/ppermute | solution.py:352
  57.5 1.9 %collective-permute-start.6 = (f32[24,1024]{1,0:T(8,128)S(1)}, f32[24,1024]{1,0:T(8,128)S(1)}, u32[]{:S(2)}, u32[]{:S(2)}) collective-permute-start(f32[24,1024]{1,0:T(8,128)S(1)} %get-tuple-element.27), channel_id=1, source_target_pairs={{0,126},{2,4},{4,2},{6,8},{8,6},{10,12},{12,10},{14,16},{16,14},{1... | collective-permute-start | bytes 294920 | tf_op jit(solution)/shard_map/ppermute | solution.py:353
  59.4 10.6 %shard_map.57 = (f32[24,1024]{1,0:T(8,128)S(1)}, bf16[48,768,256]{2,1,0:T(8,128)(2,1)S(1)}) custom-call(s32[384]{0:T(512)S(1)} %get-tuple-element.23.tab, f32[32,1024]{1,0:T(8,128)S(1)} %shard_map.55.own, f32[32,1024]{1,0:T(8,128)S(1)} %collective-permute-done.1.xa, f32[32,1024]{1,0:T(8,128)S(1)} %collective-permute-done.2.xb, ...), custom_call_target="tpu_custom_call", output_to_operand_aliasing={{1}: (4, {})} | custom-call | tf_op jit(solution)/shard_map/pallas_call | solution.py:319
  73.9 4.8 %shard_map.59 = (f32[4,24,1024]{2,1,0:T(8,128)S(1)}, f32[2,24,1024]{2,1,0:T(8,128)S(1)}) custom-call(s32[384]{0:T(512)S(1)} %get-tuple-element.23.tab, f32[24,1024]{1,0:T(8,128)S(1)} %shard_map.58.own, bf16[48,768,256]{2,1,0:T(8,128)(2,1)S(1)} %get-tuple-element.28.tens), custom_call_target="tpu_custom_call" | custom-call | tf_op jit(solution)/shard_map/pallas_call | solution.py:330
  78.8 6.0 %shard_map.61 = (f32[24,1024]{1,0:T(8,128)S(1)}, f32[24,1024]{1,0:T(8,128)S(1)}) custom-call(s32[384]{0:T(512)S(1)} %get-tuple-element.23.tab, f32[24,1024]{1,0:T(8,128)S(1)} %collective-permute-done.7.xa, f32[24,1024]{1,0:T(8,128)S(1)} %collective-permute-done.8.xb, bf16[48,768,256]{2,1,0:T(8,128)(2,1)S(1)} %get-tuple-element.28.tens, ...), custom_call_target="tpu_custom_call" | custom-call | tf_op jit(solution)/shard_map/pallas_call | solution.py:333
  88.6 3.8 %shard_map.60.field = f32[24,1024]{1,0:T(8,128)S(1)} custom-call(s32[384]{0:T(512)S(1)} %get-tuple-element.23.tab, f32[24,1024]{1,0:T(8,128)S(1)} %collective-permute-done.7.xa, f32[24,1024]{1,0:T(8,128)S(1)} %collective-permute-done.8.xb, bf16[48,768,256]{2,1,0:T(8,128)(2,1)S(1)} %get-tuple-element.28.tens, f32[2,24,1024]{2,1,0:T(8,128)S(1)} %get-tuple-element.29.acc_in), custom_call_target="tpu_custom_call" | custom-call | tf_op jit(solution)/shard_map/pallas_call | solution.py:337
  92.5 2.9 %collective-permute-done.10.from_b = f32[24,1024]{1,0:T(8,128)S(1)} collective-permute-done((f32[24,1024]{1,0:T(8,128)S(1)}, f32[24,1024]{1,0:T(8,128)S(1)}, u32[]{:S(2)}, u32[]{:S(2)}) %collective-permute-start.10) | collective-permute-done | bytes 98336 | tf_op jit(solution)/shard_map/ppermute | solution.py:353
  97.4 1.9 %collective-permute-start.11 = (f32[24,1024]{1,0:T(8,128)S(1)}, f32[24,1024]{1,0:T(8,128)S(1)}, u32[]{:S(2)}, u32[]{:S(2)}) collective-permute-start(f32[24,1024]{1,0:T(8,128)S(1)} %shard_map.62.own), channel_id=1, source_target_pairs={{0,128},{128,0},{256,384},{384,256},{1,129},{129,1},{257,385},{385... | collective-permute-start | bytes 294920 | tf_op jit(solution)/shard_map/ppermute | solution.py:43
  99.3 4.8 %shard_map.63 = (f32[4,24,1024]{2,1,0:T(8,128)S(1)}, f32[2,24,1024]{2,1,0:T(8,128)S(1)}) custom-call(s32[384]{0:T(512)S(1)} %get-tuple-element.23.tab, f32[24,1024]{1,0:T(8,128)S(1)} %shard_map.62.own, bf16[48,768,256]{2,1,0:T(8,128)(2,1)S(1)} %get-tuple-element.28.tens), custom_call_target="tpu_custom_call" | custom-call | tf_op jit(solution)/shard_map/pallas_call | solution.py:330
  104.2 6.0 %shard_map.65 = (f32[24,1024]{1,0:T(8,128)S(1)}, f32[24,1024]{1,0:T(8,128)S(1)}) custom-call(s32[384]{0:T(512)S(1)} %get-tuple-element.23.tab, f32[24,1024]{1,0:T(8,128)S(1)} %collective-permute-done.11.xa, f32[24,1024]{1,0:T(8,128)S(1)} %collective-permute-done.12.xb, bf16[48,768,256]{2,1,0:T(8,128)(2,1)S(1)} %get-tuple-element.28.tens, ...), custom_call_target="tpu_custom_call" | custom-call | tf_op jit(solution)/shard_map/pallas_call | solution.py:333
  114.1 3.8 %shard_map.64.field = f32[24,1024]{1,0:T(8,128)S(1)} custom-call(s32[384]{0:T(512)S(1)} %get-tuple-element.23.tab, f32[24,1024]{1,0:T(8,128)S(1)} %collective-permute-done.11.xa, f32[24,1024]{1,0:T(8,128)S(1)} %collective-permute-done.12.xb, bf16[48,768,256]{2,1,0:T(8,128)(2,1)S(1)} %get-tuple-element.28.tens, f32[2,24,1024]{2,1,0:T(8,128)S(1)} %get-tuple-element.33.acc_in), custom_call_target="tpu_custom_call" | custom-call | tf_op jit(solution)/shard_map/pallas_call | solution.py:337
  117.9 2.9 %collective-permute-done.14.from_b = f32[24,1024]{1,0:T(8,128)S(1)} collective-permute-done((f32[24,1024]{1,0:T(8,128)S(1)}, f32[24,1024]{1,0:T(8,128)S(1)}, u32[]{:S(2)}, u32[]{:S(2)}) %collective-permute-start.14) | collective-permute-done | bytes 98336 | tf_op jit(solution)/shard_map/ppermute | solution.py:353
  122.8 1.9 %collective-permute-start.15 = (f32[24,1024]{1,0:T(8,128)S(1)}, f32[24,1024]{1,0:T(8,128)S(1)}, u32[]{:S(2)}, u32[]{:S(2)}) collective-permute-start(f32[24,1024]{1,0:T(8,128)S(1)} %shard_map.66.own), channel_id=1, source_target_pairs={{0,128},{128,0},{256,384},{384,256},{1,129},{129,1},{257,385},{385... | collective-permute-start | bytes 294920 | tf_op jit(solution)/shard_map/ppermute | solution.py:43
  124.7 4.8 %shard_map.67 = (f32[4,24,1024]{2,1,0:T(8,128)S(1)}, f32[2,24,1024]{2,1,0:T(8,128)S(1)}) custom-call(s32[384]{0:T(512)S(1)} %get-tuple-element.23.tab, f32[24,1024]{1,0:T(8,128)S(1)} %shard_map.66.own, bf16[48,768,256]{2,1,0:T(8,128)(2,1)S(1)} %get-tuple-element.28.tens), custom_call_target="tpu_custom_call" | custom-call | tf_op jit(solution)/shard_map/pallas_call | solution.py:330
  129.6 6.0 %shard_map.69 = (f32[24,1024]{1,0:T(8,128)S(1)}, f32[24,1024]{1,0:T(8,128)S(1)}) custom-call(s32[384]{0:T(512)S(1)} %get-tuple-element.23.tab, f32[24,1024]{1,0:T(8,128)S(1)} %collective-permute-done.15.xa, f32[24,1024]{1,0:T(8,128)S(1)} %collective-permute-done.16.xb, bf16[48,768,256]{2,1,0:T(8,128)(2,1)S(1)} %get-tuple-element.28.tens, ...), custom_call_target="tpu_custom_call" | custom-call | tf_op jit(solution)/shard_map/pallas_call | solution.py:333
  139.5 3.8 %shard_map.68.field = f32[24,1024]{1,0:T(8,128)S(1)} custom-call(s32[384]{0:T(512)S(1)} %get-tuple-element.23.tab, f32[24,1024]{1,0:T(8,128)S(1)} %collective-permute-done.15.xa, f32[24,1024]{1,0:T(8,128)S(1)} %collective-permute-done.16.xb, bf16[48,768,256]{2,1,0:T(8,128)(2,1)S(1)} %get-tuple-element.28.tens, f32[2,24,1024]{2,1,0:T(8,128)S(1)} %get-tuple-element.37.acc_in), custom_call_target="tpu_custom_call" | custom-call | tf_op jit(solution)/shard_map/pallas_call | solution.py:337
  143.3 2.9 %collective-permute-done.18.from_b = f32[24,1024]{1,0:T(8,128)S(1)} collective-permute-done((f32[24,1024]{1,0:T(8,128)S(1)}, f32[24,1024]{1,0:T(8,128)S(1)}, u32[]{:S(2)}, u32[]{:S(2)}) %collective-permute-start.18) | collective-permute-done | bytes 98336 | tf_op jit(solution)/shard_map/ppermute | solution.py:353
  146.4 8.2 %collective-permute-start.19 = (f32[2,2,3,1024]{3,1,2,0:T(2,128)S(1)}, f32[2,2,3,1024]{3,1,2,0:T(2,128)S(1)}, u32[]{:S(2)}, u32[]{:S(2)}) collective-permute-start(f32[2,2,3,1024]{3,1,2,0:T(2,128)S(1)} %bitcast.31), channel_id=1, source_target_pairs={{0,1},{1,0},{2,3},{3,2},{4,5},{5,4},{6,7},{7,6},{8,9},{9,8},{10,11... | collective-permute-start | bytes 147464 | tf_op jit(solution)/shard_map/ppermute | solution.py:343
  (71 shorter events, 29.0 us)
Async XLA Ops:
  3.8 3.5 %collective-permute-start = (f32[20,1024]{1,0:T(8,128)S(1)}, f32[20,1024]{1,0:T(8,128)S(1)}, u32[]{:S(2)}, u32[]{:S(2)}) collective-permute-start(f32[20,1024]{1,0:T(8,128)S(1)} %pad_maximum_fusion), channel_id=1, source_target_pairs={{0,1},{1,0},{2,3},{3,2},{4,5},{5,4},{6,7},{7,6},{8,9},{9,8},{10,11... | collective-permute-start | bytes 245768 | tf_op jit(solution)/shard_map/ppermute | solution.py:283
  8.1 23.3 %collective-permute-start.4 = (f32[8,1024]{1,0:T(8,128)S(1)}, f32[8,1024]{1,0:T(8,128)S(1)}, u32[]{:S(2)}, u32[]{:S(2)}) collective-permute-start(f32[8,1024]{1,0:T(8,128)S(1)} %maximum_maximum_fusion.pos), channel_id=1, source_target_pairs={{0,126},{2,4},{4,2},{6,8},{8,6},{10,12},{12,10},{14,16},{16,14},{1... | collective-permute-start | bytes 98312 | tf_op jit(solution)/shard_map/ppermute | solution.py:44
  21.7 9.7 %collective-permute-start.3 = (f32[8,1024]{1,0:T(8,128)S(1)}, f32[8,1024]{1,0:T(8,128)S(1)}, u32[]{:S(2)}, u32[]{:S(2)}) collective-permute-start(f32[8,1024]{1,0:T(8,128)S(1)} %maximum_maximum_fusion.pos), channel_id=1, source_target_pairs={{0,2},{2,0},{4,6},{6,4},{8,10},{10,8},{12,14},{14,12},{16,18},{18,... | collective-permute-start | bytes 98312 | tf_op jit(solution)/shard_map/ppermute | solution.py:43
  24.1 7.3 %collective-permute-start.2 = (f32[32,1024]{1,0:T(8,128)S(1)}, f32[32,1024]{1,0:T(8,128)S(1)}, u32[]{:S(2)}, u32[]{:S(2)}) collective-permute-start(f32[32,1024]{1,0:T(8,128)S(1)} %shard_map.55.own), channel_id=1, source_target_pairs={{0,384},{128,256},{256,128},{384,0},{1,385},{129,257},{257,129},{3... | collective-permute-start | bytes 393224 | tf_op jit(solution)/shard_map/ppermute | solution.py:44
  27.2 6.1 %collective-permute-start.1 = (f32[32,1024]{1,0:T(8,128)S(1)}, f32[32,1024]{1,0:T(8,128)S(1)}, u32[]{:S(2)}, u32[]{:S(2)}) collective-permute-start(f32[32,1024]{1,0:T(8,128)S(1)} %shard_map.55.own), channel_id=1, source_target_pairs={{0,128},{128,0},{256,384},{384,256},{1,129},{129,1},{257,385},{385... | collective-permute-start | bytes 393224 | tf_op jit(solution)/shard_map/ppermute | solution.py:43
  55.5 14.4 %collective-permute-start.5 = (f32[24,1024]{1,0:T(8,128)S(1)}, f32[24,1024]{1,0:T(8,128)S(1)}, u32[]{:S(2)}, u32[]{:S(2)}) collective-permute-start(f32[24,1024]{1,0:T(8,128)S(1)} %get-tuple-element.26), channel_id=1, source_target_pairs={{0,2},{2,0},{4,6},{6,4},{8,10},{10,8},{12,14},{14,12},{16,18},{18,... | collective-permute-start | bytes 294920 | tf_op jit(solution)/shard_map/ppermute | solution.py:352
  57.5 12.5 %collective-permute-start.6 = (f32[24,1024]{1,0:T(8,128)S(1)}, f32[24,1024]{1,0:T(8,128)S(1)}, u32[]{:S(2)}, u32[]{:S(2)}) collective-permute-start(f32[24,1024]{1,0:T(8,128)S(1)} %get-tuple-element.27), channel_id=1, source_target_pairs={{0,126},{2,4},{4,2},{6,8},{8,6},{10,12},{12,10},{14,16},{16,14},{1... | collective-permute-start | bytes 294920 | tf_op jit(solution)/shard_map/ppermute | solution.py:353
  70.0 8.7 %collective-permute-start.8 = (f32[24,1024]{1,0:T(8,128)S(1)}, f32[24,1024]{1,0:T(8,128)S(1)}, u32[]{:S(2)}, u32[]{:S(2)}) collective-permute-start(f32[24,1024]{1,0:T(8,128)S(1)} %shard_map.58.own), channel_id=1, source_target_pairs={{0,384},{128,256},{256,128},{384,0},{1,385},{129,257},{257,129},{3... | collective-permute-start | bytes 294920 | tf_op jit(solution)/shard_map/ppermute | solution.py:44
  72.0 6.8 %collective-permute-start.7 = (f32[24,1024]{1,0:T(8,128)S(1)}, f32[24,1024]{1,0:T(8,128)S(1)}, u32[]{:S(2)}, u32[]{:S(2)}) collective-permute-start(f32[24,1024]{1,0:T(8,128)S(1)} %shard_map.58.own), channel_id=1, source_target_pairs={{0,128},{128,0},{256,384},{384,256},{1,129},{129,1},{257,385},{385... | collective-permute-start | bytes 294920 | tf_op jit(solution)/shard_map/ppermute | solution.py:43
  84.8 7.7 %collective-permute-start.9 = (f32[24,1024]{1,0:T(8,128)S(1)}, f32[24,1024]{1,0:T(8,128)S(1)}, u32[]{:S(2)}, u32[]{:S(2)}) collective-permute-start(f32[24,1024]{1,0:T(8,128)S(1)} %get-tuple-element.31), channel_id=1, source_target_pairs={{0,2},{2,0},{4,6},{6,4},{8,10},{10,8},{12,14},{14,12},{16,18},{18,... | collective-permute-start | bytes 294920 | tf_op jit(solution)/shard_map/ppermute | solution.py:352
  86.7 8.7 %collective-permute-start.10 = (f32[24,1024]{1,0:T(8,128)S(1)}, f32[24,1024]{1,0:T(8,128)S(1)}, u32[]{:S(2)}, u32[]{:S(2)}) collective-permute-start(f32[24,1024]{1,0:T(8,128)S(1)} %get-tuple-element.32), channel_id=1, source_target_pairs={{0,126},{2,4},{4,2},{6,8},{8,6},{10,12},{12,10},{14,16},{16,14},{1... | collective-permute-start | bytes 294920 | tf_op jit(solution)/shard_map/ppermute | solution.py:353
  95.5 8.7 %collective-permute-start.12 = (f32[24,1024]{1,0:T(8,128)S(1)}, f32[24,1024]{1,0:T(8,128)S(1)}, u32[]{:S(2)}, u32[]{:S(2)}) collective-permute-start(f32[24,1024]{1,0:T(8,128)S(1)} %shard_map.62.own), channel_id=1, source_target_pairs={{0,384},{128,256},{256,128},{384,0},{1,385},{129,257},{257,129},{3... | collective-permute-start | bytes 294920 | tf_op jit(solution)/shard_map/ppermute | solution.py:44
  97.4 6.8 %collective-permute-start.11 = (f32[24,1024]{1,0:T(8,128)S(1)}, f32[24,1024]{1,0:T(8,128)S(1)}, u32[]{:S(2)}, u32[]{:S(2)}) collective-permute-start(f32[24,1024]{1,0:T(8,128)S(1)} %shard_map.62.own), channel_id=1, source_target_pairs={{0,128},{128,0},{256,384},{384,256},{1,129},{129,1},{257,385},{385... | collective-permute-start | bytes 294920 | tf_op jit(solution)/shard_map/ppermute | solution.py:43
  110.2 7.7 %collective-permute-start.13 = (f32[24,1024]{1,0:T(8,128)S(1)}, f32[24,1024]{1,0:T(8,128)S(1)}, u32[]{:S(2)}, u32[]{:S(2)}) collective-permute-start(f32[24,1024]{1,0:T(8,128)S(1)} %get-tuple-element.35), channel_id=1, source_target_pairs={{0,2},{2,0},{4,6},{6,4},{8,10},{10,8},{12,14},{14,12},{16,18},{18,... | collective-permute-start | bytes 294920 | tf_op jit(solution)/shard_map/ppermute | solution.py:352
  112.1 8.7 %collective-permute-start.14 = (f32[24,1024]{1,0:T(8,128)S(1)}, f32[24,1024]{1,0:T(8,128)S(1)}, u32[]{:S(2)}, u32[]{:S(2)}) collective-permute-start(f32[24,1024]{1,0:T(8,128)S(1)} %get-tuple-element.36), channel_id=1, source_target_pairs={{0,126},{2,4},{4,2},{6,8},{8,6},{10,12},{12,10},{14,16},{16,14},{1... | collective-permute-start | bytes 294920 | tf_op jit(solution)/shard_map/ppermute | solution.py:353
  120.9 8.7 %collective-permute-start.16 = (f32[24,1024]{1,0:T(8,128)S(1)}, f32[24,1024]{1,0:T(8,128)S(1)}, u32[]{:S(2)}, u32[]{:S(2)}) collective-permute-start(f32[24,1024]{1,0:T(8,128)S(1)} %shard_map.66.own), channel_id=1, source_target_pairs={{0,384},{128,256},{256,128},{384,0},{1,385},{129,257},{257,129},{3... | collective-permute-start | bytes 294920 | tf_op jit(solution)/shard_map/ppermute | solution.py:44
  122.8 6.8 %collective-permute-start.15 = (f32[24,1024]{1,0:T(8,128)S(1)}, f32[24,1024]{1,0:T(8,128)S(1)}, u32[]{:S(2)}, u32[]{:S(2)}) collective-permute-start(f32[24,1024]{1,0:T(8,128)S(1)} %shard_map.66.own), channel_id=1, source_target_pairs={{0,128},{128,0},{256,384},{384,256},{1,129},{129,1},{257,385},{385... | collective-permute-start | bytes 294920 | tf_op jit(solution)/shard_map/ppermute | solution.py:43
  135.6 7.7 %collective-permute-start.17 = (f32[24,1024]{1,0:T(8,128)S(1)}, f32[24,1024]{1,0:T(8,128)S(1)}, u32[]{:S(2)}, u32[]{:S(2)}) collective-permute-start(f32[24,1024]{1,0:T(8,128)S(1)} %get-tuple-element.39), channel_id=1, source_target_pairs={{0,2},{2,0},{4,6},{6,4},{8,10},{10,8},{12,14},{14,12},{16,18},{18,... | collective-permute-start | bytes 294920 | tf_op jit(solution)/shard_map/ppermute | solution.py:352
  137.5 8.7 %collective-permute-start.18 = (f32[24,1024]{1,0:T(8,128)S(1)}, f32[24,1024]{1,0:T(8,128)S(1)}, u32[]{:S(2)}, u32[]{:S(2)}) collective-permute-start(f32[24,1024]{1,0:T(8,128)S(1)} %get-tuple-element.40), channel_id=1, source_target_pairs={{0,126},{2,4},{4,2},{6,8},{8,6},{10,12},{12,10},{14,16},{16,14},{1... | collective-permute-start | bytes 294920 | tf_op jit(solution)/shard_map/ppermute | solution.py:353
  146.4 9.1 %collective-permute-start.19 = (f32[2,2,3,1024]{3,1,2,0:T(2,128)S(1)}, f32[2,2,3,1024]{3,1,2,0:T(2,128)S(1)}, u32[]{:S(2)}, u32[]{:S(2)}) collective-permute-start(f32[2,2,3,1024]{3,1,2,0:T(2,128)S(1)} %bitcast.31), channel_id=1, source_target_pairs={{0,1},{1,0},{2,3},{3,2},{4,5},{5,4},{6,7},{7,6},{8,9},{9,8},{10,11... | collective-permute-start | bytes 147464 | tf_op jit(solution)/shard_map/ppermute | solution.py:343

commit v2 on v1

v2 whole, which is shorter than its diff:
```python
import functools
import math

import jax
import jax.numpy as jnp
from jax import lax
from jax.experimental import pallas as pl
from jax.experimental.pallas import tpu as pltpu
from jax.sharding import PartitionSpec as P

BLOCK = 128
ITERS = 4

cell_width = 4.0
coupling = 0.8
root_pi = 1.0 / math.sqrt(math.pi)
erfcx_fit = (
    1.790011536,
    0.928601473,
    0.3238769782,
    0.05183749415,
    -0.01103335474,
    -0.006028563159,
    0.0006207049413,
    0.0006951546236,
    -6.044884693e-05,
    -6.930253734e-05,
)

VMEM = pl.BlockSpec(memory_space=pltpu.VMEM)
SMEM = pl.BlockSpec(memory_space=pltpu.SMEM)


def swaps(count, first):
    if first:
        return [(i, i ^ 1) for i in range(count)]
    return [(i, (i + 1) % count if i % 2 else (i - 1) % count) for i in range(count)]


def exchange(value, axis):
    count = lax.axis_size(axis)
    return (
        lax.ppermute(value, axis, swaps(count, True)),
        lax.ppermute(value, axis, swaps(count, False)),
    )


def rows_of(value, block):
    return value[:, pl.ds(pl.multiple_of(block * BLOCK, BLOCK), BLOCK)]


def lower_half(shape):
    return lax.broadcasted_iota(jnp.int32, shape, 0) % 8 < 4


def build(word, spos, tpos, tens):
    entry = word & 63
    src_block = (word >> 6) & 7
    half = (word >> 9) & 1
    tgt_block = (word >> 10) & 7
    tgt_half = (word >> 13) & 1
    tgt_slot = (word >> 14) & 3
    shift_x = (((word >> 16) & 3) - 1).astype(jnp.float32) * -cell_width
    shift_y = (((word >> 18) & 3) - 1).astype(jnp.float32) * cell_width
    src_slot = (word >> 20) & 3
    src = spos.at[src_slot * 2 + half]
    src_cols = pl.ds(pl.multiple_of(src_block * BLOCK, BLOCK), BLOCK)
    tgt_cols = pl.ds(pl.multiple_of(tgt_block * BLOCK, BLOCK), BLOCK)
    tgt = tpos.at[tgt_slot * 2 + tgt_half]
    tx, ty, tz = (tgt[k : k + 1, tgt_cols] for k in range(3))
    source = jnp.transpose(src[:, src_cols])
    chunk = 32
    for start in range(0, BLOCK, chunk):
        part = source[start : start + chunk]
        dx = tx - part[:, 0:1] + shift_x
        dy = ty - part[:, 1:2] + shift_y
        dz = tz - part[:, 2:3]
        dist_sq = dx * dx + dy * dy + dz * dz + 1.0
        inv_dist = lax.rsqrt(dist_sq)
        distance = dist_sq * inv_dist
        inv_sq = inv_dist * inv_dist
        reach = 1.0 / (distance + 4.0)
        at = reach * 10.0 - 1.0
        fit = jnp.full_like(at, erfcx_fit[-1])
        for coef in erfcx_fit[-2::-1]:
            fit = fit * at + coef
        decay = jnp.exp(dist_sq * -0.25)
        b_term = inv_sq * decay * (fit * reach * inv_dist + root_pi)
        c_term = inv_sq * (3.0 * b_term + (0.5 * root_pi) * decay)
        cx, cy, cz = c_term * dx, c_term * dy, c_term * dz
        comps = (cx * dx - b_term, cx * dy, cx * dz, cy * dy - b_term, cy * dz, cz * dz - b_term)
        for k, comp in enumerate(comps):
            high = comp.astype(jnp.bfloat16)
            low = (comp - high.astype(jnp.float32)).astype(jnp.bfloat16)
            cols = slice(k * BLOCK, (k + 1) * BLOCK)
            tens[entry, start : start + chunk, cols] = high
            tens[entry, BLOCK + start : BLOCK + start + chunk, cols] = low


def apply(words, counts, dips, tens, out):
    results = []
    for word, live in zip(words, counts):
        entry = word & 63
        src_block = (word >> 6) & 7
        half = (word >> 9) & 1
        cols = pl.ds(pl.multiple_of(src_block * BLOCK, BLOCK), BLOCK)
        row_half = lax.broadcasted_iota(jnp.int32, (8, BLOCK), 0) % 8 // 4
        src_slot = (word >> 20) & 3
        mine = row_half == half
        left, right = [], []
        for k in range(3):
            value = dips[src_slot, 8 * k : 8 * k + 8, cols]
            if live is not None:
                value = jnp.where(live, value, 0.0)
            high = value.astype(jnp.bfloat16).astype(jnp.float32)
            low = pltpu.roll(value - high, 4, 0)
            left.append(jnp.where(mine, high, low))
            right.append(jnp.where(mine, high, 0.0))
        lhs = jnp.concatenate(
            [jnp.concatenate(left, axis=0), jnp.concatenate(right, axis=0)], axis=1
        ).astype(jnp.bfloat16)
        results.append(
            lax.dot_general(
                lhs, tens[entry], (((1,), (0,)), ((), ())), preferred_element_type=jnp.float32
            )
        )
    pick = ((0, 1, 2), (1, 3, 4), (2, 4, 5))
    for word, res in zip(words, results):
        tgt_block = (word >> 10) & 7
        tgt_half = (word >> 13) & 1
        outcols = pl.ds(pl.multiple_of(tgt_block * BLOCK, BLOCK), BLOCK)
        for a in range(3):
            total = res[0:8, pick[a][0] * BLOCK : (pick[a][0] + 1) * BLOCK]
            for b in (1, 2):
                k = pick[a][b]
                total = total + res[8 * b : 8 * b + 8, k * BLOCK : (k + 1) * BLOCK]
            out[tgt_half, 8 * a : 8 * a + 8, outcols] += total


def each_build(tab, group, spos, tpos, tens):
    base = group * 64
    count = tab[base]

    def step(i, carry):
        for j in range(2):
            build(tab[base + 1 + jnp.minimum(2 * i + j, count - 1)], spos, tpos, tens)
        return carry

    lax.fori_loop(0, (count + 1) // 2, step, 0)


def each_apply(tab, group, dips, tens, out):
    base = group * 64
    count = tab[base]

    def step(i, carry):
        words, live = [], []
        for j in range(4):
            at = 4 * i + j
            words.append(tab[base + 1 + jnp.minimum(at, count - 1)])
            live.append(None if j == 0 else at < count)
        apply(words, live, dips, tens, out)
        return carry

    lax.fori_loop(0, (count + 3) // 4, step, 0)


def settle(acc, out):
    for a in range(3):
        rows = slice(8 * a, 8 * a + 8)
        own, other = acc[0, rows, :], acc[1, rows, :]
        own = own + pltpu.roll(own, 4, 0)
        other = other + pltpu.roll(other, 4, 0)
        out[rows, :] = jnp.where(lower_half(own.shape), own, other)


def sort_entries(lists, tab):
    for group in range(6):
        tab[group * 64] = 0
    core, even_x, even_y = lists[50], lists[51], lists[52]
    for half in range(2):

        def place(p, carry, half=half):
            code = lists[half * 25 + p]
            steps = code >> 7
            step_x = (steps * 11) >> 5
            step_y = steps - 3 * step_x
            slot_x = jnp.where(step_x == 1, 0, jnp.where((step_x == 2) == (even_x == 1), 1, 2))
            slot_y = jnp.where(step_y == 1, 0, jnp.where((step_y == 2) == (even_y == 1), 1, 2))
            tgt_half = ((code >> 6) & 1) ^ core
            word = (
                (half * 24 + p)
                | ((code & 7) << 6)
                | (half << 9)
                | (((code >> 3) & 7) << 10)
                | (tgt_half << 13)
                | (slot_y << 14)
                | (step_x << 16)
                | (step_y << 18)
                | (slot_x << 20)
            )
            group = slot_y + jnp.where(slot_x == 0, 0, 3)
            at = tab[group * 64]
            tab[group * 64 + 1 + at] = word
            tab[group * 64] = at + 1
            return carry

        lax.fori_loop(0, lists[half * 25 + 24], place, 0)


def stack_dipoles(dips, arrays):
    for slot, value in arrays:
        dips[slot] = value[0:24, :]


def stack_positions(place, arrays):
    for slot, value, row in arrays:
        for half in range(2):
            place[slot * 2 + half, 0:3, :] = value[row + 3 * half : row + 3 * half + 3, :]


def first_local_kernel(lists, own, ya, yb, tens, tab, here, at_a, at_b, dips, spos, tpos):
    sort_entries(lists, tab)
    stack_dipoles(dips, ((0, own),))
    stack_positions(spos, ((0, own, 24),))
    stack_positions(tpos, ((0, own, 24), (1, ya, 0), (2, yb, 0)))
    for group in range(3):
        each_build(tab, group, spos, tpos, tens)
    for group, out in enumerate((here, at_a, at_b)):
        out[...] = jnp.zeros_like(out)
        each_apply(tab, group, dips, tens, out)


def local_kernel(tab, own, tens, here, at_a, at_b, dips):
    stack_dipoles(dips, ((0, own),))
    for group, out in enumerate((here, at_a, at_b)):
        out[...] = jnp.zeros_like(out)
        each_apply(tab, group, dips, tens, out)


def first_rest_kernel(group, tab, xa, xb, target, tens_in, begun, out, tens, dips, spos, tpos, acc):
    stack_dipoles(dips, ((1, xa), (2, xb)))
    stack_positions(spos, ((1, xa, 24), (2, xb, 24)))
    stack_positions(tpos, ((group, target, 0 if group else 24),))
    acc[...] = begun[...]
    each_build(tab, 3 + group, spos, tpos, tens)
    each_apply(tab, 3 + group, dips, tens, acc)
    settle(acc, out)


def rest_kernel(group, tab, xa, xb, tens, begun, out, dips, acc):
    stack_dipoles(dips, ((1, xa), (2, xb)))
    acc[...] = begun[...]
    each_apply(tab, 3 + group, dips, tens, acc)
    settle(acc, out)


def respond_rows(alpha, total):
    real_row = lax.broadcasted_iota(jnp.int32, (8, total.shape[1]), 0) % 4 < 2
    turned = jnp.where(real_row, pltpu.roll(total, 6, 0), pltpu.roll(total, 2, 0))
    return alpha[0:8] * total + alpha[8:16] * turned


def update_kernel(field, from_a, from_b, applied, alpha, dip):
    for a in range(3):
        rows = slice(8 * a, 8 * a + 8)
        total = applied[rows, :] + coupling * (field[rows, :] + from_a[rows, :] + from_b[rows, :])
        dip[rows, :] = respond_rows(alpha[...], total)


def last_kernel(field, from_a, from_b, applied, alpha, kept, passed):
    for a in range(3):
        rows = slice(8 * a, 8 * a + 8)
        total = applied[rows, :] + coupling * (field[rows, :] + from_a[rows, :] + from_b[rows, :])
        dip = respond_rows(alpha[...], total)
        for i in range(2):
            for f in range(2):
                at = 2 * i + f
                kept[f, i, a : a + 1, :] = dip[at : at + 1]
                passed[f, i, a : a + 1, :] = dip[4 + at : 5 + at]


def pack_kernel(lists, positions, polarizability, applied, sent, mine):
    core = lists[25]
    for out, first in ((mine, 2 * core), (sent, 2 - 2 * core)):
        for i in range(2):
            for f in range(2):
                for a in range(3):
                    row = 4 * a + 2 * i + f
                    out[row : row + 1, :] = applied[first + f, i, a : a + 1, :]
                row = 12 + 2 * i + f
                out[row : row + 1, :] = polarizability[first + f, i : i + 1, :]
    sent[16:19, :] = positions[...]
    lane = lax.broadcasted_iota(jnp.int32, (1, BLOCK), 1)
    codes = jnp.zeros((1, BLOCK), jnp.int32)
    for p in range(25):
        codes = jnp.where(lane == p, lists[p], codes)
    sent[19:24, :] = jnp.zeros((5, sent.shape[1]), jnp.float32)
    sent[19:20, 0:BLOCK] = codes.astype(jnp.float32)


def join_kernel(mine, got, positions, applied, alpha, pos, own):
    for half, value in enumerate((mine, got)):
        for a in range(3):
            applied[8 * a + 4 * half : 8 * a + 4 * half + 4, :] = value[4 * a : 4 * a + 4, :]
        real, imag = value[12:14, :], value[14:16, :]
        alpha[4 * half : 4 * half + 2, :] = real
        alpha[4 * half + 2 : 4 * half + 4, :] = real
        alpha[8 + 4 * half : 10 + 4 * half, :] = -imag
        alpha[10 + 4 * half : 12 + 4 * half, :] = imag
    pos[0:3, :] = positions[...]
    pos[3:6, :] = got[16:19, :]
    pos[6:8, :] = jnp.zeros((2, pos.shape[1]), jnp.float32)
    for a in range(3):
        rows = slice(8 * a, 8 * a + 8)
        own[rows, :] = respond_rows(alpha[...], applied[rows, :])
    own[24:32, :] = pos[...]


def call(body, out_shape, scratch=(), in_specs=None, out_specs=None, aliases=None):
    specs = {} if in_specs is None else {"in_specs": in_specs, "out_specs": out_specs}
    return pl.pallas_call(
        body,
        out_shape=out_shape,
        **specs,
        scratch_shapes=list(scratch),
        input_output_aliases=aliases or {},
        compiler_params=pltpu.CompilerParams(vmem_limit_bytes=16 * 1024 * 1024),
    )


def shards(positions, polarizability, applied_field, pair_codes, pair_counts):
    rows = positions.shape[1]
    entries = pair_codes.shape[0]
    core = lax.axis_index("gz")
    f32 = jnp.float32
    arr = lambda *shape: jax.ShapeDtypeStruct((*shape, rows), f32)
    held = lambda *shape: pltpu.VMEM((*shape, rows), f32)
    parity = lambda axis: 1 - lax.axis_index(axis) % 2
    turn = lambda value, first: lax.ppermute(value, "gy", swaps(lax.axis_size("gy"), first))
    codes = jnp.concatenate([pair_codes, pair_counts])
    place = jnp.stack([core, parity("gx"), parity("gy")]).astype(jnp.int32)
    sent, mine = call(
        pack_kernel, (arr(24), arr(16)), (), [SMEM] + [VMEM] * 3, (VMEM, VMEM)
    )(jnp.concatenate([codes, place]), positions, polarizability, applied_field)
    got = lax.ppermute(sent, "gz", swaps(2, True))
    applied, alpha, pos, own = call(join_kernel, (arr(24), arr(16), arr(8), arr(32)))(
        mine, got, positions
    )
    lists = jnp.concatenate([codes, got[19, : entries + 1].astype(jnp.int32), place])
    yb = turn(pos, False)
    ya = turn(pos, True)
    xa, xb = exchange(own, "gx")
    tens_shape = pltpu.VMEM((2 * entries, 2 * BLOCK, 6 * BLOCK), jnp.bfloat16)
    keep = lambda v: pltpu.with_memory_space_constraint(v, pltpu.VMEM)
    tab_shape = jax.ShapeDtypeStruct((6 * 64,), jnp.int32)
    dip_scratch, pos_scratch, acc_scratch = held(3, 24), held(6, 8), held(2, 24)
    sums = (arr(2, 24),) * 3
    tens, tab, here, at_a, at_b = call(
        first_local_kernel,
        (tens_shape, tab_shape, *sums),
        (dip_scratch, pos_scratch, pos_scratch),
        [SMEM] + [VMEM] * 3,
        (VMEM, SMEM, VMEM, VMEM, VMEM),
    )(lists, own, ya, yb)

    def first_rest(group, target, tens, begun):
        return call(
            functools.partial(first_rest_kernel, group),
            (arr(24), tens_shape),
            (dip_scratch, pos_scratch, pos_scratch, acc_scratch),
            [SMEM] + [VMEM] * 5,
            (VMEM, VMEM),
            {4: 1},
        )(tab, xa, xb, target, keep(tens), begun)

    def rest(group, xa, xb, begun):
        return call(
            functools.partial(rest_kernel, group),
            arr(24),
            (dip_scratch, acc_scratch),
            [SMEM] + [VMEM] * 4,
            VMEM,
        )(tab, xa, xb, keep(tens), begun)

    msg_b, tens = first_rest(2, yb, tens, at_b)
    from_b = turn(msg_b, False)
    msg_a, tens = first_rest(1, ya, tens, at_a)
    from_a = turn(msg_a, True)
    field, tens = first_rest(0, own, tens, here)
    for sweep in range(1, ITERS):
        dip = call(update_kernel, arr(24))(field, from_a, from_b, applied, alpha)
        xa, xb = exchange(dip, "gx")
        here, at_a, at_b = call(
            local_kernel, sums, (dip_scratch,), [SMEM] + [VMEM] * 2, (VMEM,) * 3
        )(tab, dip, keep(tens))
        from_b = turn(rest(2, xa, xb, at_b), False)
        from_a = turn(rest(1, xa, xb, at_a), True)
        field = rest(0, xa, xb, here)
    half = jax.ShapeDtypeStruct((2, 2, 3, rows), f32)
    kept, passed = call(last_kernel, (half, half))(field, from_a, from_b, applied, alpha)
    passed = lax.ppermute(passed, "gz", swaps(2, True))
    return jnp.where(
        core == 0, jnp.concatenate([kept, passed]), jnp.concatenate([passed, kept])
    )


def solution(mesh):
    in_specs = (
        P(None, ("gx", "gy", "gz")),
        P(None, None, ("gx", "gy", "gz")),
        P(None, None, None, ("gx", "gy", "gz")),
        P(("gx", "gy", "gz")),
        P(("gx", "gy", "gz")),
    )
    out_specs = P(None, None, None, ("gx", "gy", "gz"))
    return jax.shard_map(shards, mesh=mesh, in_specs=in_specs, out_specs=out_specs, check_vma=False)
```

time: 157 us -> 138 us (0.88)
  the two profiles are of different devices: /device:TPU:3 before, /device:TPU:1 now
where the time goes in v2:
time: 138 us; the launch traced here: 137 us
  starting transfers between devices  94 us (68%)
  Pallas kernels  23.1 us (17%)
  waiting for transfers between devices  14.5 us (11%)
  local copies, waits for them, and re-layouts  4.62 us (3%)
    ppermute x10, starting transfers between devices, shards(): lax.ppermute(value, 'gy', swaps(lax.axis_size('gy'), first))  46.5 us
    ppermute x4, starting transfers between devices, exchange(): lax.ppermute(value, axis, swaps(count, False))  18.2 us
    ppermute x1, starting transfers between devices, shards(): passed = lax.ppermute(passed, 'gz', swaps(2, True))  12.8 us
    ppermute x1, starting transfers between devices, shards(): got = lax.ppermute(sent, 'gz', swaps(2, True))  8.79 us
    pallas_call x9, Pallas kernels, rest(): call(functools.partial(rest_kernel, group), arr(24), (dip_scratch, acc_sc...  7.77 us
    ppermute x4, starting transfers between devices, exchange(): lax.ppermute(value, axis, swaps(count, True))  7.68 us
    ppermute x10, waiting for transfers between devices, shards(): lax.ppermute(value, 'gy', swaps(lax.axis_size('gy'), first))  7.58 us
    pallas_call x3, Pallas kernels, shards(): call(local_kernel, sums, (dip_scratch,), [SMEM] + [VMEM] * 2, (VMEM,) * 3)  5.18 us
  transfers between devices with their start and end apart: 20, of which 10 were waited for; matrix products, arithmetic and copies ran while one was open for 1% of the time, Pallas kernels for 12%

profile of v2, /device:TPU:1, one launch (start us, length us, event | category | flops | bytes accessed | tf_op | source)
XLA Modules:
  0.0 137.3 jit_solution(4190448952693842344)
XLA Ops:
  4.4 8.8 %collective-permute-start = (f32[24,1024]{1,0:T(8,128)S(1)}, f32[24,1024]{1,0:T(8,128)S(1)}, u32[]{:S(2)}, u32[]{:S(2)}) collective-permute-start(f32[24,1024]{1,0:T(8,128)S(1)} %get-tuple-element.33), channel_id=1, source_target_pairs={{0,1},{1,0},{2,3},{3,2},{4,5},{5,4},{6,7},{7,6},{8,9},{9,8},{10,11... | collective-permute-start | bytes 294920 | tf_op jit(solution)/shard_map/ppermute | solution.py:346
  14.2 8.2 %collective-permute-start.2 = (f32[8,1024]{1,0:T(8,128)S(1)}, f32[8,1024]{1,0:T(8,128)S(1)}, u32[]{:S(2)}, u32[]{:S(2)}) collective-permute-start(f32[8,1024]{1,0:T(8,128)S(1)} %get-tuple-element.36), channel_id=1, source_target_pairs={{0,126},{2,4},{4,2},{6,8},{8,6},{10,12},{12,10},{14,16},{16,14},{1... | collective-permute-start | bytes 98312 | tf_op jit(solution)/shard_map/ppermute | solution.py:340
  22.4 1.9 %collective-permute-start.1 = (f32[8,1024]{1,0:T(8,128)S(1)}, f32[8,1024]{1,0:T(8,128)S(1)}, u32[]{:S(2)}, u32[]{:S(2)}) collective-permute-start(f32[8,1024]{1,0:T(8,128)S(1)} %get-tuple-element.36), channel_id=1, source_target_pairs={{0,2},{2,0},{4,6},{6,4},{8,10},{10,8},{12,14},{14,12},{16,18},{18,... | collective-permute-start | bytes 98312 | tf_op jit(solution)/shard_map/ppermute | solution.py:340
  24.3 4.4 %collective-permute-start.4 = (f32[32,1024]{1,0:T(8,128)S(1)}, f32[32,1024]{1,0:T(8,128)S(1)}, u32[]{:S(2)}, u32[]{:S(2)}) collective-permute-start(f32[32,1024]{1,0:T(8,128)S(1)} %get-tuple-element.35.own.target), channel_id=1, source_target_pairs={{0,384},{128,256},{256,128},{384,0},{1,385},{129,257},{257,129},{3... | collective-permute-start | bytes 393224 | tf_op jit(solution)/shard_map/ppermute | solution.py:44
  28.7 1.9 %collective-permute-start.3 = (f32[32,1024]{1,0:T(8,128)S(1)}, f32[32,1024]{1,0:T(8,128)S(1)}, u32[]{:S(2)}, u32[]{:S(2)}) collective-permute-start(f32[32,1024]{1,0:T(8,128)S(1)} %get-tuple-element.35.own.target), channel_id=1, source_target_pairs={{0,128},{128,0},{256,384},{384,256},{1,129},{129,1},{257,385},{385... | collective-permute-start | bytes 393224 | tf_op jit(solution)/shard_map/ppermute | solution.py:43
  31.4 4.9 %shard_map.57 = (bf16[48,256,768]{2,1,0:T(8,128)(2,1)S(1)}, s32[384]{0:T(512)S(1)}, f32[2,24,1024]{2,1,0:T(8,128)S(1)}, f32[2,24,1024]{2,1,0:T(8,128)S(1)}, f32[2,24,1024]{2,1,0:T(8,128)S(1)}) custom-call(s32[53]{0:T(128)S(1)} %concatenate.16.lists, f32[32,1024]{1,0:T(8,128)S(1)} %get-tuple-element.35.own.target, ...), custom_call_target="tpu_custom_call" | custom-call | tf_op jit(solution)/shard_map/pallas_call | solution.py:359
  38.6 2.3 %collective-permute-start.5 = (f32[24,1024]{1,0:T(8,128)S(1)}, f32[24,1024]{1,0:T(8,128)S(1)}, u32[]{:S(2)}, u32[]{:S(2)}) collective-permute-start(f32[24,1024]{1,0:T(8,128)S(1)} %get-tuple-element.45), channel_id=1, source_target_pairs={{0,2},{2,0},{4,6},{6,4},{8,10},{10,8},{12,14},{14,12},{16,18},{18,... | collective-permute-start | bytes 294920 | tf_op jit(solution)/shard_map/ppermute | solution.py:340
  41.0 11.1 %collective-permute-start.6 = (f32[24,1024]{1,0:T(8,128)S(1)}, f32[24,1024]{1,0:T(8,128)S(1)}, u32[]{:S(2)}, u32[]{:S(2)}) collective-permute-start(f32[24,1024]{1,0:T(8,128)S(1)} %get-tuple-element.46), channel_id=1, source_target_pairs={{0,126},{2,4},{4,2},{6,8},{8,6},{10,12},{12,10},{14,16},{16,14},{1... | collective-permute-start | bytes 294920 | tf_op jit(solution)/shard_map/ppermute | solution.py:340
  52.1 2.2 %shard_map.60 = (f32[24,1024]{1,0:T(8,128)S(1)}, bf16[48,256,768]{2,1,0:T(8,128)(2,1)S(1)}) custom-call(s32[384]{0:T(512)S(1)} %get-tuple-element.37.tab, f32[32,1024]{1,0:T(8,128)S(1)} %collective-permute-done.3.xa, f32[32,1024]{1,0:T(8,128)S(1)} %collective-permute-done.4.xb, ...), custom_call_target="tpu_custom_call", output_to_operand_aliasing={{1}: (4, {})} | custom-call | tf_op jit(solution)/shard_map/pallas_call | solution.py:368
  54.3 7.2 %collective-permute-start.8 = (f32[24,1024]{1,0:T(8,128)S(1)}, f32[24,1024]{1,0:T(8,128)S(1)}, u32[]{:S(2)}, u32[]{:S(2)}) collective-permute-start(f32[24,1024]{1,0:T(8,128)S(1)} %shard_map.61.own), channel_id=1, source_target_pairs={{0,384},{128,256},{256,128},{384,0},{1,385},{129,257},{257,129},{3... | collective-permute-start | bytes 294920 | tf_op jit(solution)/shard_map/ppermute | solution.py:44
  61.6 1.9 %collective-permute-start.7 = (f32[24,1024]{1,0:T(8,128)S(1)}, f32[24,1024]{1,0:T(8,128)S(1)}, u32[]{:S(2)}, u32[]{:S(2)}) collective-permute-start(f32[24,1024]{1,0:T(8,128)S(1)} %shard_map.61.own), channel_id=1, source_target_pairs={{0,128},{128,0},{256,384},{384,256},{1,129},{129,1},{257,385},{385... | collective-permute-start | bytes 294920 | tf_op jit(solution)/shard_map/ppermute | solution.py:43
  67.9 6.3 %collective-permute-start.10 = (f32[24,1024]{1,0:T(8,128)S(1)}, f32[24,1024]{1,0:T(8,128)S(1)}, u32[]{:S(2)}, u32[]{:S(2)}) collective-permute-start(f32[24,1024]{1,0:T(8,128)S(1)} %shard_map.65), channel_id=1, source_target_pairs={{0,126},{2,4},{4,2},{6,8},{8,6},{10,12},{12,10},{14,16},{16,14},{1... | collective-permute-start | bytes 294920 | tf_op jit(solution)/shard_map/ppermute | solution.py:340
  74.9 1.9 %collective-permute-start.9 = (f32[24,1024]{1,0:T(8,128)S(1)}, f32[24,1024]{1,0:T(8,128)S(1)}, u32[]{:S(2)}, u32[]{:S(2)}) collective-permute-start(f32[24,1024]{1,0:T(8,128)S(1)} %shard_map.64), channel_id=1, source_target_pairs={{0,2},{2,0},{4,6},{6,4},{8,10},{10,8},{12,14},{14,12},{16,18},{18,... | collective-permute-start | bytes 294920 | tf_op jit(solution)/shard_map/ppermute | solution.py:340
  77.8 2.7 %collective-permute-done.9.from_a = f32[24,1024]{1,0:T(8,128)S(1)} collective-permute-done((f32[24,1024]{1,0:T(8,128)S(1)}, f32[24,1024]{1,0:T(8,128)S(1)}, u32[]{:S(2)}, u32[]{:S(2)}) %collective-permute-start.9) | collective-permute-done | bytes 98336 | tf_op jit(solution)/shard_map/ppermute | solution.py:340
  80.6 2.1 %collective-permute-start.12 = (f32[24,1024]{1,0:T(8,128)S(1)}, f32[24,1024]{1,0:T(8,128)S(1)}, u32[]{:S(2)}, u32[]{:S(2)}) collective-permute-start(f32[24,1024]{1,0:T(8,128)S(1)} %shard_map.66.own), channel_id=1, source_target_pairs={{0,384},{128,256},{256,128},{384,0},{1,385},{129,257},{257,129},{3... | collective-permute-start | bytes 294920 | tf_op jit(solution)/shard_map/ppermute | solution.py:44
  82.6 1.9 %collective-permute-start.11 = (f32[24,1024]{1,0:T(8,128)S(1)}, f32[24,1024]{1,0:T(8,128)S(1)}, u32[]{:S(2)}, u32[]{:S(2)}) collective-permute-start(f32[24,1024]{1,0:T(8,128)S(1)} %shard_map.66.own), channel_id=1, source_target_pairs={{0,128},{128,0},{256,384},{384,256},{1,129},{129,1},{257,385},{385... | collective-permute-start | bytes 294920 | tf_op jit(solution)/shard_map/ppermute | solution.py:43
  89.0 4.2 %collective-permute-start.14 = (f32[24,1024]{1,0:T(8,128)S(1)}, f32[24,1024]{1,0:T(8,128)S(1)}, u32[]{:S(2)}, u32[]{:S(2)}) collective-permute-start(f32[24,1024]{1,0:T(8,128)S(1)} %shard_map.70), channel_id=1, source_target_pairs={{0,126},{2,4},{4,2},{6,8},{8,6},{10,12},{12,10},{14,16},{16,14},{1... | collective-permute-start | bytes 294920 | tf_op jit(solution)/shard_map/ppermute | solution.py:340
  93.8 1.9 %collective-permute-start.13 = (f32[24,1024]{1,0:T(8,128)S(1)}, f32[24,1024]{1,0:T(8,128)S(1)}, u32[]{:S(2)}, u32[]{:S(2)}) collective-permute-start(f32[24,1024]{1,0:T(8,128)S(1)} %shard_map.69), channel_id=1, source_target_pairs={{0,2},{2,0},{4,6},{6,4},{8,10},{10,8},{12,14},{14,12},{16,18},{18,... | collective-permute-start | bytes 294920 | tf_op jit(solution)/shard_map/ppermute | solution.py:340
  99.2 4.6 %collective-permute-start.16 = (f32[24,1024]{1,0:T(8,128)S(1)}, f32[24,1024]{1,0:T(8,128)S(1)}, u32[]{:S(2)}, u32[]{:S(2)}) collective-permute-start(f32[24,1024]{1,0:T(8,128)S(1)} %shard_map.71.own), channel_id=1, source_target_pairs={{0,384},{128,256},{256,128},{384,0},{1,385},{129,257},{257,129},{3... | collective-permute-start | bytes 294920 | tf_op jit(solution)/shard_map/ppermute | solution.py:44
  103.8 1.9 %collective-permute-start.15 = (f32[24,1024]{1,0:T(8,128)S(1)}, f32[24,1024]{1,0:T(8,128)S(1)}, u32[]{:S(2)}, u32[]{:S(2)}) collective-permute-start(f32[24,1024]{1,0:T(8,128)S(1)} %shard_map.71.own), channel_id=1, source_target_pairs={{0,128},{128,0},{256,384},{384,256},{1,129},{129,1},{257,385},{385... | collective-permute-start | bytes 294920 | tf_op jit(solution)/shard_map/ppermute | solution.py:43
  110.1 6.6 %collective-permute-start.18 = (f32[24,1024]{1,0:T(8,128)S(1)}, f32[24,1024]{1,0:T(8,128)S(1)}, u32[]{:S(2)}, u32[]{:S(2)}) collective-permute-start(f32[24,1024]{1,0:T(8,128)S(1)} %shard_map.75), channel_id=1, source_target_pairs={{0,126},{2,4},{4,2},{6,8},{8,6},{10,12},{12,10},{14,16},{16,14},{1... | collective-permute-start | bytes 294920 | tf_op jit(solution)/shard_map/ppermute | solution.py:340
  117.4 1.9 %collective-permute-start.17 = (f32[24,1024]{1,0:T(8,128)S(1)}, f32[24,1024]{1,0:T(8,128)S(1)}, u32[]{:S(2)}, u32[]{:S(2)}) collective-permute-start(f32[24,1024]{1,0:T(8,128)S(1)} %shard_map.74), channel_id=1, source_target_pairs={{0,2},{2,0},{4,6},{6,4},{8,10},{10,8},{12,14},{14,12},{16,18},{18,... | collective-permute-start | bytes 294920 | tf_op jit(solution)/shard_map/ppermute | solution.py:340
  120.3 2.4 %collective-permute-done.17.from_a = f32[24,1024]{1,0:T(8,128)S(1)} collective-permute-done((f32[24,1024]{1,0:T(8,128)S(1)}, f32[24,1024]{1,0:T(8,128)S(1)}, u32[]{:S(2)}, u32[]{:S(2)}) %collective-permute-start.17) | collective-permute-done | bytes 98336 | tf_op jit(solution)/shard_map/ppermute | solution.py:340
  122.8 12.8 %collective-permute-start.19 = (f32[2,2,3,1024]{3,2,1,0:T(4,128)S(1)}, f32[2,2,3,1024]{3,2,1,0:T(4,128)S(1)}, u32[]{:S(2)}, u32[]{:S(2)}) collective-permute-start(f32[2,2,3,1024]{3,2,1,0:T(4,128)S(1)} %get-tuple-element.60), channel_id=1, source_target_pairs={{0,1},{1,0},{2,3},{3,2},{4,5},{5,4},{6,7},{7,6},{8,9},{9,8},{10,11... | collective-permute-start | bytes 147464 | tf_op jit(solution)/shard_map/ppermute | solution.py:402
  (48 shorter events, 30.0 us)
Async XLA Ops:
  2.3 0.7 copy-start
  3.1 0.8 copy-start.1
  4.4 9.7 %collective-permute-start = (f32[24,1024]{1,0:T(8,128)S(1)}, f32[24,1024]{1,0:T(8,128)S(1)}, u32[]{:S(2)}, u32[]{:S(2)}) collective-permute-start(f32[24,1024]{1,0:T(8,128)S(1)} %get-tuple-element.33), channel_id=1, source_target_pairs={{0,1},{1,0},{2,3},{3,2},{4,5},{5,4},{6,7},{7,6},{8,9},{9,8},{10,11... | collective-permute-start | bytes 294920 | tf_op jit(solution)/shard_map/ppermute | solution.py:346
  14.2 17.2 %collective-permute-start.2 = (f32[8,1024]{1,0:T(8,128)S(1)}, f32[8,1024]{1,0:T(8,128)S(1)}, u32[]{:S(2)}, u32[]{:S(2)}) collective-permute-start(f32[8,1024]{1,0:T(8,128)S(1)} %get-tuple-element.36), channel_id=1, source_target_pairs={{0,126},{2,4},{4,2},{6,8},{8,6},{10,12},{12,10},{14,16},{16,14},{1... | collective-permute-start | bytes 98312 | tf_op jit(solution)/shard_map/ppermute | solution.py:340
  22.4 9.0 %collective-permute-start.1 = (f32[8,1024]{1,0:T(8,128)S(1)}, f32[8,1024]{1,0:T(8,128)S(1)}, u32[]{:S(2)}, u32[]{:S(2)}) collective-permute-start(f32[8,1024]{1,0:T(8,128)S(1)} %get-tuple-element.36), channel_id=1, source_target_pairs={{0,2},{2,0},{4,6},{6,4},{8,10},{10,8},{12,14},{14,12},{16,18},{18,... | collective-permute-start | bytes 98312 | tf_op jit(solution)/shard_map/ppermute | solution.py:340
  24.3 12.0 %collective-permute-start.4 = (f32[32,1024]{1,0:T(8,128)S(1)}, f32[32,1024]{1,0:T(8,128)S(1)}, u32[]{:S(2)}, u32[]{:S(2)}) collective-permute-start(f32[32,1024]{1,0:T(8,128)S(1)} %get-tuple-element.35.own.target), channel_id=1, source_target_pairs={{0,384},{128,256},{256,128},{384,0},{1,385},{129,257},{257,129},{3... | collective-permute-start | bytes 393224 | tf_op jit(solution)/shard_map/ppermute | solution.py:44
  28.7 7.6 %collective-permute-start.3 = (f32[32,1024]{1,0:T(8,128)S(1)}, f32[32,1024]{1,0:T(8,128)S(1)}, u32[]{:S(2)}, u32[]{:S(2)}) collective-permute-start(f32[32,1024]{1,0:T(8,128)S(1)} %get-tuple-element.35.own.target), channel_id=1, source_target_pairs={{0,128},{128,0},{256,384},{384,256},{1,129},{129,1},{257,385},{385... | collective-permute-start | bytes 393224 | tf_op jit(solution)/shard_map/ppermute | solution.py:43
  38.6 15.6 %collective-permute-start.5 = (f32[24,1024]{1,0:T(8,128)S(1)}, f32[24,1024]{1,0:T(8,128)S(1)}, u32[]{:S(2)}, u32[]{:S(2)}) collective-permute-start(f32[24,1024]{1,0:T(8,128)S(1)} %get-tuple-element.45), channel_id=1, source_target_pairs={{0,2},{2,0},{4,6},{6,4},{8,10},{10,8},{12,14},{14,12},{16,18},{18,... | collective-permute-start | bytes 294920 | tf_op jit(solution)/shard_map/ppermute | solution.py:340
  41.0 13.3 %collective-permute-start.6 = (f32[24,1024]{1,0:T(8,128)S(1)}, f32[24,1024]{1,0:T(8,128)S(1)}, u32[]{:S(2)}, u32[]{:S(2)}) collective-permute-start(f32[24,1024]{1,0:T(8,128)S(1)} %get-tuple-element.46), channel_id=1, source_target_pairs={{0,126},{2,4},{4,2},{6,8},{8,6},{10,12},{12,10},{14,16},{16,14},{1... | collective-permute-start | bytes 294920 | tf_op jit(solution)/shard_map/ppermute | solution.py:340
  54.3 10.9 %collective-permute-start.8 = (f32[24,1024]{1,0:T(8,128)S(1)}, f32[24,1024]{1,0:T(8,128)S(1)}, u32[]{:S(2)}, u32[]{:S(2)}) collective-permute-start(f32[24,1024]{1,0:T(8,128)S(1)} %shard_map.61.own), channel_id=1, source_target_pairs={{0,384},{128,256},{256,128},{384,0},{1,385},{129,257},{257,129},{3... | collective-permute-start | bytes 294920 | tf_op jit(solution)/shard_map/ppermute | solution.py:44
  61.6 5.4 %collective-permute-start.7 = (f32[24,1024]{1,0:T(8,128)S(1)}, f32[24,1024]{1,0:T(8,128)S(1)}, u32[]{:S(2)}, u32[]{:S(2)}) collective-permute-start(f32[24,1024]{1,0:T(8,128)S(1)} %shard_map.61.own), channel_id=1, source_target_pairs={{0,128},{128,0},{256,384},{384,256},{1,129},{129,1},{257,385},{385... | collective-permute-start | bytes 294920 | tf_op jit(solution)/shard_map/ppermute | solution.py:43
  67.9 9.9 %collective-permute-start.10 = (f32[24,1024]{1,0:T(8,128)S(1)}, f32[24,1024]{1,0:T(8,128)S(1)}, u32[]{:S(2)}, u32[]{:S(2)}) collective-permute-start(f32[24,1024]{1,0:T(8,128)S(1)} %shard_map.65), channel_id=1, source_target_pairs={{0,126},{2,4},{4,2},{6,8},{8,6},{10,12},{12,10},{14,16},{16,14},{1... | collective-permute-start | bytes 294920 | tf_op jit(solution)/shard_map/ppermute | solution.py:340
  74.9 5.7 %collective-permute-start.9 = (f32[24,1024]{1,0:T(8,128)S(1)}, f32[24,1024]{1,0:T(8,128)S(1)}, u32[]{:S(2)}, u32[]{:S(2)}) collective-permute-start(f32[24,1024]{1,0:T(8,128)S(1)} %shard_map.64), channel_id=1, source_target_pairs={{0,2},{2,0},{4,6},{6,4},{8,10},{10,8},{12,14},{14,12},{16,18},{18,... | collective-permute-start | bytes 294920 | tf_op jit(solution)/shard_map/ppermute | solution.py:340
  80.6 6.6 %collective-permute-start.12 = (f32[24,1024]{1,0:T(8,128)S(1)}, f32[24,1024]{1,0:T(8,128)S(1)}, u32[]{:S(2)}, u32[]{:S(2)}) collective-permute-start(f32[24,1024]{1,0:T(8,128)S(1)} %shard_map.66.own), channel_id=1, source_target_pairs={{0,384},{128,256},{256,128},{384,0},{1,385},{129,257},{257,129},{3... | collective-permute-start | bytes 294920 | tf_op jit(solution)/shard_map/ppermute | solution.py:44
  82.6 5.4 %collective-permute-start.11 = (f32[24,1024]{1,0:T(8,128)S(1)}, f32[24,1024]{1,0:T(8,128)S(1)}, u32[]{:S(2)}, u32[]{:S(2)}) collective-permute-start(f32[24,1024]{1,0:T(8,128)S(1)} %shard_map.66.own), channel_id=1, source_target_pairs={{0,128},{128,0},{256,384},{384,256},{1,129},{129,1},{257,385},{385... | collective-permute-start | bytes 294920 | tf_op jit(solution)/shard_map/ppermute | solution.py:43
  89.0 8.7 %collective-permute-start.14 = (f32[24,1024]{1,0:T(8,128)S(1)}, f32[24,1024]{1,0:T(8,128)S(1)}, u32[]{:S(2)}, u32[]{:S(2)}) collective-permute-start(f32[24,1024]{1,0:T(8,128)S(1)} %shard_map.70), channel_id=1, source_target_pairs={{0,126},{2,4},{4,2},{6,8},{8,6},{10,12},{12,10},{14,16},{16,14},{1... | collective-permute-start | bytes 294920 | tf_op jit(solution)/shard_map/ppermute | solution.py:340
  93.8 5.4 %collective-permute-start.13 = (f32[24,1024]{1,0:T(8,128)S(1)}, f32[24,1024]{1,0:T(8,128)S(1)}, u32[]{:S(2)}, u32[]{:S(2)}) collective-permute-start(f32[24,1024]{1,0:T(8,128)S(1)} %shard_map.69), channel_id=1, source_target_pairs={{0,2},{2,0},{4,6},{6,4},{8,10},{10,8},{12,14},{14,12},{16,18},{18,... | collective-permute-start | bytes 294920 | tf_op jit(solution)/shard_map/ppermute | solution.py:340
  99.2 8.3 %collective-permute-start.16 = (f32[24,1024]{1,0:T(8,128)S(1)}, f32[24,1024]{1,0:T(8,128)S(1)}, u32[]{:S(2)}, u32[]{:S(2)}) collective-permute-start(f32[24,1024]{1,0:T(8,128)S(1)} %shard_map.71.own), channel_id=1, source_target_pairs={{0,384},{128,256},{256,128},{384,0},{1,385},{129,257},{257,129},{3... | collective-permute-start | bytes 294920 | tf_op jit(solution)/shard_map/ppermute | solution.py:44
  103.8 5.4 %collective-permute-start.15 = (f32[24,1024]{1,0:T(8,128)S(1)}, f32[24,1024]{1,0:T(8,128)S(1)}, u32[]{:S(2)}, u32[]{:S(2)}) collective-permute-start(f32[24,1024]{1,0:T(8,128)S(1)} %shard_map.71.own), channel_id=1, source_target_pairs={{0,128},{128,0},{256,384},{384,256},{1,129},{129,1},{257,385},{385... | collective-permute-start | bytes 294920 | tf_op jit(solution)/shard_map/ppermute | solution.py:43
  110.1 10.2 %collective-permute-start.18 = (f32[24,1024]{1,0:T(8,128)S(1)}, f32[24,1024]{1,0:T(8,128)S(1)}, u32[]{:S(2)}, u32[]{:S(2)}) collective-permute-start(f32[24,1024]{1,0:T(8,128)S(1)} %shard_map.75), channel_id=1, source_target_pairs={{0,126},{2,4},{4,2},{6,8},{8,6},{10,12},{12,10},{14,16},{16,14},{1... | collective-permute-start | bytes 294920 | tf_op jit(solution)/shard_map/ppermute | solution.py:340
  117.4 5.4 %collective-permute-start.17 = (f32[24,1024]{1,0:T(8,128)S(1)}, f32[24,1024]{1,0:T(8,128)S(1)}, u32[]{:S(2)}, u32[]{:S(2)}) collective-permute-start(f32[24,1024]{1,0:T(8,128)S(1)} %shard_map.74), channel_id=1, source_target_pairs={{0,2},{2,0},{4,6},{6,4},{8,10},{10,8},{12,14},{14,12},{16,18},{18,... | collective-permute-start | bytes 294920 | tf_op jit(solution)/shard_map/ppermute | solution.py:340
  122.8 13.7 %collective-permute-start.19 = (f32[2,2,3,1024]{3,2,1,0:T(4,128)S(1)}, f32[2,2,3,1024]{3,2,1,0:T(4,128)S(1)}, u32[]{:S(2)}, u32[]{:S(2)}) collective-permute-start(f32[2,2,3,1024]{3,2,1,0:T(4,128)S(1)} %get-tuple-element.60), channel_id=1, source_target_pairs={{0,1},{1,0},{2,3},{3,2},{4,5},{5,4},{6,7},{7,6},{8,9},{9,8},{10,11... | collective-permute-start | bytes 147464 | tf_op jit(solution)/shard_map/ppermute | solution.py:402

commit v3 on v2

v3 whole, which is shorter than its diff:
```python
import functools
import math

import jax
import jax.numpy as jnp
from jax import lax
from jax.experimental import pallas as pl
from jax.experimental.pallas import tpu as pltpu
from jax.sharding import PartitionSpec as P

BLOCK = 128
ITERS = 4

cell_width = 4.0
coupling = 0.8
root_pi = 1.0 / math.sqrt(math.pi)
erfcx_fit = (
    1.790011536,
    0.928601473,
    0.3238769782,
    0.05183749415,
    -0.01103335474,
    -0.006028563159,
    0.0006207049413,
    0.0006951546236,
    -6.044884693e-05,
    -6.930253734e-05,
)

VMEM = pl.BlockSpec(memory_space=pltpu.VMEM)
SMEM = pl.BlockSpec(memory_space=pltpu.SMEM)
SLABS = 4
KEPT = 72
STRIDE = 256


def swaps(count, first):
    if first:
        return [(i, i ^ 1) for i in range(count)]
    return [(i, (i + 1) % count if i % 2 else (i - 1) % count) for i in range(count)]


def columns(block):
    return pl.ds(pl.multiple_of(block * BLOCK, BLOCK), BLOCK)


def build(word, src_pos, tgt_pos, tens, slot):
    src_slab = (word >> 11) & 3
    tgt_slab = (word >> 16) & 3
    shift_x = (((word >> 18) & 3) - 1).astype(jnp.float32) * -cell_width
    shift_y = (((word >> 20) & 3) - 1).astype(jnp.float32) * cell_width
    tgt_cols = columns((word >> 13) & 7)
    tx, ty, tz = (tgt_pos[tgt_slab, k : k + 1, tgt_cols] for k in range(3))
    tx, ty = tx + shift_x, ty + shift_y
    source = jnp.transpose(src_pos[src_slab, :, columns((word >> 8) & 7)])
    chunk = 32
    for start in range(0, BLOCK, chunk):
        part = source[start : start + chunk]
        dx = tx - part[:, 0:1]
        dy = ty - part[:, 1:2]
        dz = tz - part[:, 2:3]
        dist_sq = dx * dx + dy * dy + dz * dz + 1.0
        inv_dist = lax.rsqrt(dist_sq)
        distance = dist_sq * inv_dist
        inv_sq = inv_dist * inv_dist
        reach = 1.0 / (distance + 4.0)
        at = reach * 10.0 - 1.0
        fit = jnp.full_like(at, erfcx_fit[-1])
        for coef in erfcx_fit[-2::-1]:
            fit = fit * at + coef
        decay = jnp.exp2(dist_sq * (-0.25 / math.log(2.0)))
        b_term = inv_sq * decay * (fit * reach * inv_dist + root_pi)
        c_term = inv_sq * (3.0 * b_term + (0.5 * root_pi) * decay)
        cx, cy, cz = c_term * dx, c_term * dy, c_term * dz
        comps = (cx * dx - b_term, cx * dy, cx * dz, cy * dy - b_term, cy * dz, cz * dz - b_term)
        for k, comp in enumerate(comps):
            high = comp.astype(jnp.bfloat16)
            low = (comp - high.astype(jnp.float32)).astype(jnp.bfloat16)
            cols = slice(k * BLOCK, (k + 1) * BLOCK)
            tens[slot, start : start + chunk, cols] = high
            tens[slot, BLOCK + start : BLOCK + start + chunk, cols] = low


def apply(words, slots, live, dip, tens, out):
    results = []
    row_slab = lax.broadcasted_iota(jnp.int32, (8, BLOCK), 0) // 2
    for word, slot, ok in zip(words, slots, live):
        src_slab = (word >> 11) & 3
        cols = columns((word >> 8) & 7)
        mine = row_slab == src_slab
        beside = row_slab == ((src_slab + 1) & 3)
        left, right = [], []
        for k in range(3):
            value = dip[8 * k : 8 * k + 8, cols]
            if ok is not None:
                value = jnp.where(ok, value, 0.0)
            high = value.astype(jnp.bfloat16).astype(jnp.float32)
            low = pltpu.roll(value - high, 2, 0)
            part = jnp.where(mine, high, 0.0)
            left.append(jnp.where(beside, low, part))
            right.append(part)
        lhs = jnp.concatenate(
            [jnp.concatenate(left, axis=0), jnp.concatenate(right, axis=0)], axis=1
        ).astype(jnp.bfloat16)
        results.append(
            lax.dot_general(
                lhs, tens[slot], (((1,), (0,)), ((), ())), preferred_element_type=jnp.float32
            )
        )
    pick = ((0, 1, 2), (1, 3, 4), (2, 4, 5))
    for word, res in zip(words, results):
        cols = columns((word >> 13) & 7)
        tgt_slab = (word >> 16) & 3
        for a in range(3):
            total = res[0:8, pick[a][0] * BLOCK : (pick[a][0] + 1) * BLOCK]
            for b in (1, 2):
                k = pick[a][b]
                total = total + res[8 * b : 8 * b + 8, k * BLOCK : (k + 1) * BLOCK]
            out[tgt_slab, 8 * a : 8 * a + 8, cols] += total


def each_build(tab, group, src_pos, tgt_pos, tens):
    base = group * STRIDE
    count = tab[base]

    def step(i, carry):
        for j in range(2):
            word = tab[base + 1 + jnp.minimum(2 * i + j, count - 1)]
            build(word, src_pos, tgt_pos, tens, word & 255)
        return carry

    lax.fori_loop(0, (count + 1) // 2, step, 0)


def each_apply(tab, group, dip, tens, out):
    base = group * STRIDE
    count = tab[base]

    def step(i, carry):
        words, live = [], []
        for j in range(4):
            at = 4 * i + j
            words.append(tab[base + 1 + jnp.minimum(at, count - 1)])
            live.append(None if j == 0 else at < count)
        apply(words, [word & 255 for word in words], live, dip, tens, out)
        return carry

    lax.fori_loop(0, (count + 3) // 4, step, 0)


def each_other(tab, group, src_pos, tgt_pos, dip, out, one):
    base = (group + 6) * STRIDE

    def step(i, carry):
        word = tab[base + 1 + i]
        build(word, src_pos, tgt_pos, one, 0)
        apply([word], [0], [None], dip, one, out)
        return carry

    lax.fori_loop(0, tab[base], step, 0)


def settle(acc, out):
    for a in range(3):
        rows = slice(8 * a, 8 * a + 8)
        joined = None
        for s in range(SLABS):
            part = acc[s, rows, :]
            part = part + pltpu.roll(part, 4, 0)
            part = part + pltpu.roll(part, 2, 0)
            mine = lax.broadcasted_iota(jnp.int32, part.shape, 0) // 2 == s
            joined = part if s == 0 else jnp.where(mine, part, joined)
        out[rows, :] = joined


def sort_entries(lists, tab):
    for group in range(12):
        tab[group * STRIDE] = 0
    core = lax.axis_index("gz")
    odd_y = lax.rem(lax.axis_index("gy"), 2)
    used = jnp.int32(0)
    for half in range(2):
        for slab in range(SLABS):
            which = half * SLABS + slab

            def place(p, used, half=half, slab=slab, which=which):
                code = lists[which, 0, p].astype(jnp.int32)
                steps = code >> 7
                step_x = (steps * 11) >> 5
                step_y = steps - 3 * step_x
                slot_y = jnp.where(step_y == 1, 0, jnp.where((step_y == 2) == (odd_y == 0), 1, 2))
                word = (
                    used
                    | ((code & 7) << 8)
                    | (((slab + step_x + SLABS - 1) & (SLABS - 1)) << 11)
                    | (((code >> 3) & 7) << 13)
                    | (slab << 16)
                    | (step_x << 18)
                    | (step_y << 20)
                )
                group = 3 * half + slot_y + jnp.where(used >= KEPT, 6, 0)
                hit = jnp.where(((code >> 6) & 1) == core, 1, 0)
                at = tab[group * STRIDE]
                tab[group * STRIDE + 1 + at] = word
                tab[group * STRIDE] = at + hit
                return used + hit

            used = lax.fori_loop(0, lists[which, 0, 24].astype(jnp.int32), place, used)


def spread(value, row, out):
    for s in range(SLABS):
        out[s, 0:3, :] = value[row + 3 * s : row + 3 * s + 3, :]


def first_kernel(own, got, tens, tab, own_pos, got_pos, lists, sems):
    copies = []
    for half, value in enumerate((own, got)):
        for s in range(SLABS):
            which = half * SLABS + s
            row = 36 + s
            copies.append(
                pltpu.make_async_copy(
                    value.at[row : row + 1, 0:BLOCK], lists.at[which], sems.at[which]
                )
            )
    for copy in copies:
        copy.start()
    own_pos[...] = jnp.zeros_like(own_pos)
    got_pos[...] = jnp.zeros_like(got_pos)
    spread(own, 24, own_pos)
    spread(got, 24, got_pos)
    for copy in copies:
        copy.wait()
    sort_entries(lists, tab)
    each_build(tab, 0, own_pos, own_pos, tens)
    each_build(tab, 3, got_pos, own_pos, tens)


def first_far_kernel(slot, tab, own, got, own_pos, got_pos, pos, tens_in, out, tens, tgt_pos, acc, one):
    spread(pos, 0, tgt_pos)
    acc[...] = jnp.zeros_like(acc)
    for group, src_pos, dip in ((slot, own_pos, own), (3 + slot, got_pos, got)):
        each_build(tab, group, src_pos, tgt_pos, tens)
        each_apply(tab, group, dip, tens, acc)
        each_other(tab, group, src_pos, tgt_pos, dip, acc, one)
    settle(acc, out)


def own_kernel(tab, own, own_pos, pos_a, pos_b, tens, at_a, at_b, tgt_pos, one):
    for slot, pos, out in ((2, pos_b, at_b), (1, pos_a, at_a)):
        out[...] = jnp.zeros_like(out)
        each_apply(tab, slot, own, tens, out)
        spread(pos, 0, tgt_pos)
        each_other(tab, slot, own_pos, tgt_pos, own, out, one)


def far_kernel(slot, tab, got, got_pos, pos, tens, begun, out, tgt_pos, acc, one):
    acc[...] = begun[...]
    each_apply(tab, 3 + slot, got, tens, acc)
    spread(pos, 0, tgt_pos)
    each_other(tab, 3 + slot, got_pos, tgt_pos, got, acc, one)
    settle(acc, out)


def here_kernel(tab, own, got, own_pos, got_pos, tens, out, acc, one):
    acc[...] = jnp.zeros_like(acc)
    for group, src_pos, dip in ((0, own_pos, own), (3, got_pos, got)):
        each_apply(tab, group, dip, tens, acc)
        each_other(tab, group, src_pos, own_pos, dip, acc, one)
    settle(acc, out)


def respond_rows(alpha, total):
    real_row = lax.broadcasted_iota(jnp.int32, (8, total.shape[1]), 0) % 2 < 1
    turned = jnp.where(real_row, pltpu.roll(total, 7, 0), pltpu.roll(total, 1, 0))
    return alpha[0:8] * total + alpha[8:16] * turned


def update_kernel(field, from_a, from_b, applied, alpha, dip):
    for a in range(3):
        rows = slice(8 * a, 8 * a + 8)
        total = applied[rows, :] + coupling * (field[rows, :] + from_a[rows, :] + from_b[rows, :])
        dip[rows, :] = respond_rows(alpha[...], total)


def last_kernel(field, from_a, from_b, applied, alpha, out):
    out[...] = jnp.zeros_like(out)
    for a in range(3):
        rows = slice(8 * a, 8 * a + 8)
        total = applied[rows, :] + coupling * (field[rows, :] + from_a[rows, :] + from_b[rows, :])
        dip = respond_rows(alpha[...], total)
        for s in range(SLABS):
            for i in range(2):
                out[s, 3 * i + a : 3 * i + a + 1, :] = dip[2 * s + i : 2 * s + i + 1]


def pack_kernel(pos, pol, field, codes, count, out):
    lane = lax.broadcasted_iota(jnp.int32, (1, BLOCK), 1)
    row = jnp.where(lane == codes.shape[0], count[0], 0)
    for p in range(codes.shape[0]):
        row = jnp.where(lane == p, codes[p], row)
    for f in range(SLABS):
        for i in range(2):
            out[f, 3 * i : 3 * i + 3, :] = field[f, i]
        out[f, 6:8, :] = pol[f]
        out[f, 8:16, :] = jnp.zeros((8, out.shape[2]), jnp.float32)
        out[f, 8:11, :] = pos[...]
        out[f, 11:12, 0:BLOCK] = row.astype(jnp.float32)


def join_kernel(got, applied, alpha, own, pos):
    for s in range(SLABS):
        for i in range(2):
            for a in range(3):
                row = 8 * a + 2 * s + i
                applied[row : row + 1, :] = got[s, 3 * i + a : 3 * i + a + 1, :]
        real, imag = got[s, 6:7, :], got[s, 7:8, :]
        alpha[2 * s : 2 * s + 1, :] = real
        alpha[2 * s + 1 : 2 * s + 2, :] = real
        alpha[8 + 2 * s : 9 + 2 * s, :] = -imag
        alpha[9 + 2 * s : 10 + 2 * s, :] = imag
        pos[3 * s : 3 * s + 3, :] = got[s, 8:11, :]
        own[24 + 3 * s : 27 + 3 * s, :] = got[s, 8:11, :]
        own[36 + s : 37 + s, :] = got[s, 11:12, :]
    for a in range(3):
        rows = slice(8 * a, 8 * a + 8)
        own[rows, :] = respond_rows(alpha[...], applied[rows, :])


def call(body, out_shape, scratch=(), in_specs=None, out_specs=None, aliases=None):
    specs = {} if in_specs is None else {"in_specs": in_specs, "out_specs": out_specs}
    return pl.pallas_call(
        body,
        out_shape=out_shape,
        **specs,
        scratch_shapes=list(scratch),
        input_output_aliases=aliases or {},
        compiler_params=pltpu.CompilerParams(vmem_limit_bytes=6 * 1024 * 1024),
    )


def shards(positions, polarizability, applied_field, pair_codes, pair_counts):
    rows = positions.shape[1]
    f32 = jnp.float32
    arr = lambda *shape: jax.ShapeDtypeStruct((*shape, rows), f32)
    held = lambda *shape: pltpu.VMEM((*shape, rows), f32)
    flip = lambda value: lax.ppermute(value, "gz", swaps(2, True))
    turn = lambda value, first: lax.ppermute(value, "gy", swaps(lax.axis_size("gy"), first))
    keep = lambda value: pltpu.with_memory_space_constraint(value, pltpu.VMEM)
    fixed = lambda value: pltpu.with_memory_space_constraint(value, pltpu.SMEM)
    sent = call(pack_kernel, arr(SLABS, 16), (), [VMEM] * 3 + [SMEM] * 2, VMEM)(
        positions, polarizability, applied_field, pair_codes, pair_counts
    )
    got = lax.all_to_all(sent, "gx", 0, 0)
    applied, alpha, own, pos = call(join_kernel, (arr(24), arr(16), arr(40), arr(12)))(got)
    got = flip(own)
    pos_b = turn(pos, False)
    pos_a = turn(pos, True)
    tens_shape = pltpu.VMEM((KEPT, 2 * BLOCK, 6 * BLOCK), jnp.bfloat16)
    one = pltpu.VMEM((1, 2 * BLOCK, 6 * BLOCK), jnp.bfloat16)
    tgt_pos, acc = held(SLABS, 8), held(SLABS, 24)
    tens, tab, own_pos, got_pos = call(
        first_kernel,
        (tens_shape, pltpu.SMEM((12 * STRIDE,), jnp.int32), arr(SLABS, 8), arr(SLABS, 8)),
        (pltpu.SMEM((2 * SLABS, 1, BLOCK), f32), pltpu.SemaphoreType.DMA((2 * SLABS,))),
        [VMEM] * 2,
        (VMEM, SMEM, VMEM, VMEM),
    )(own, got)
    tab = fixed(tab)

    def first_far(slot, pos, tens):
        return call(
            functools.partial(first_far_kernel, slot),
            (arr(24), tens_shape),
            (tgt_pos, acc, one),
            [SMEM] + [VMEM] * 6,
            (VMEM, VMEM),
            {6: 1},
        )(tab, own, got, own_pos, got_pos, pos, keep(tens))

    def here(own, got):
        return call(here_kernel, arr(24), (acc, one), [SMEM] + [VMEM] * 5, VMEM)(
            tab, own, got, own_pos, got_pos, keep(tens)
        )

    def far(slot, got, pos, begun):
        return call(
            functools.partial(far_kernel, slot),
            arr(24),
            (tgt_pos, acc, one),
            [SMEM] + [VMEM] * 5,
            VMEM,
        )(tab, got, got_pos, pos, keep(tens), begun)

    msg, tens = first_far(2, pos_b, tens)
    from_b = turn(msg, False)
    msg, tens = first_far(1, pos_a, tens)
    from_a = turn(msg, True)
    field = here(own, got)
    for sweep in range(1, ITERS):
        own = call(update_kernel, arr(24))(field, from_a, from_b, applied, alpha)
        got = flip(own)
        at_a, at_b = call(
            own_kernel,
            (arr(SLABS, 24), arr(SLABS, 24)),
            (tgt_pos, one),
            [SMEM] + [VMEM] * 5,
            (VMEM, VMEM),
        )(tab, own, own_pos, pos_a, pos_b, keep(tens))
        from_b = turn(far(2, got, pos_b, at_b), False)
        from_a = turn(far(1, got, pos_a, at_a), True)
        field = here(own, got)
    out = call(last_kernel, arr(SLABS, 8))(field, from_a, from_b, applied, alpha)
    out = lax.all_to_all(out, "gx", 0, 0)
    return out[:, :6].reshape(SLABS, 2, 3, rows)


def solution(mesh):
    in_specs = (
        P(None, ("gx", "gy", "gz")),
        P(None, None, ("gx", "gy", "gz")),
        P(None, None, None, ("gx", "gy", "gz")),
        P(("gx", "gy", "gz")),
        P(("gx", "gy", "gz")),
    )
    out_specs = P(None, None, None, ("gx", "gy", "gz"))
    return jax.shard_map(shards, mesh=mesh, in_specs=in_specs, out_specs=out_specs, check_vma=False)
```

time: 138 us -> 137 us (level)
  the two profiles are of different devices: /device:TPU:1 before, /device:TPU:248 now
where the time goes in v3:
time: 137 us; the launch traced here: 136 us
  Pallas kernels  56.3 us (41%)
  starting transfers between devices  47.4 us (35%)
  blocking collectives  19.1 us (14%)
  waiting for transfers between devices  8.65 us (6%)
  local copies, waits for them, and re-layouts  3.86 us (3%)
    ppermute x10, starting transfers between devices, shards(): lax.ppermute(value, 'gy', swaps(lax.axis_size('gy'), first))  39.7 us
    pallas_call x2, Pallas kernels, first_far(): call(functools.partial(first_far_kernel, slot), (arr(24), tens_shape), (t...  20.2 us
    all_to_all x1, blocking collectives, shards(): got = lax.all_to_all(sent, 'gx', 0, 0)  10.8 us
    pallas_call x1, Pallas kernels, shards(): call(first_kernel, (tens_shape, pltpu.SMEM((12 * STRIDE,), jnp.int32), ar...  9.77 us
    pallas_call x3, Pallas kernels, shards(): call(own_kernel, (arr(SLABS, 24), arr(SLABS, 24)), (tgt_pos, one), [SMEM]...  9.56 us
    ppermute x10, waiting for transfers between devices, shards(): lax.ppermute(value, 'gy', swaps(lax.axis_size('gy'), first))  8.64 us
    all_to_all x1, blocking collectives, shards(): out = lax.all_to_all(out, 'gx', 0, 0)  8.36 us
    pallas_call x4, Pallas kernels, here(): call(here_kernel, arr(24), (acc, one), [SMEM] + [VMEM] * 5, VMEM)  8.28 us
  transfers between devices with their start and end apart: 14, of which 5 were waited for; matrix products, arithmetic and copies ran while one was open for 0% of the time, Pallas kernels for 30%

profile of v3, /device:TPU:248, one launch (start us, length us, event | category | flops | bytes accessed | tf_op | source)
XLA Modules:
  0.0 136.3 jit_solution(1272835970294649601)
XLA Ops:
  4.3 10.8 %all_to_all.10.got = f32[4,16,1024]{2,1,0:T(8,128)S(1)} all-to-all(f32[4,16,1024]{2,1,0:T(8,128)S(1)} %shard_map.55), channel_id=1, replica_groups=mesh['gx'=4,'gy'=64,'gz'=2] {'gx'}, dimensions={0} | all-to-all | bytes 524288 | tf_op jit(solution)/shard_map/all_to_all | solution.py:355
  15.2 1.9 %collective-permute-start = (f32[40,1024]{1,0:T(8,128)S(1)}, f32[40,1024]{1,0:T(8,128)S(1)}, u32[]{:S(2)}, u32[]{:S(2)}) collective-permute-start(f32[40,1024]{1,0:T(8,128)S(1)} %get-tuple-element.23.own), channel_id=1, source_target_pairs={{0,1},{1,0},{2,3},{3,2},{4,5},{5,4},{6,7},{7,6},{8,9},{9,8},{10,11... | collective-permute-start | bytes 491528 | tf_op jit(solution)/shard_map/ppermute | solution.py:348
  17.1 4.7 %collective-permute-start.2 = (f32[12,1024]{1,0:T(8,128)S(1)}, f32[12,1024]{1,0:T(8,128)S(1)}, u32[]{:S(2)}, u32[]{:S(2)}) collective-permute-start(f32[12,1024]{1,0:T(8,128)S(1)} %get-tuple-element.27), channel_id=1, source_target_pairs={{0,126},{2,4},{4,2},{6,8},{8,6},{10,12},{12,10},{14,16},{16,14},{1... | collective-permute-start | bytes 147464 | tf_op jit(solution)/shard_map/ppermute | solution.py:349
  23.8 9.8 %shard_map.57 = (bf16[72,256,768]{2,1,0:T(8,128)(2,1)S(1)}, s32[3072]{0:T(1024)S(4)}, f32[4,8,1024]{2,1,0:T(8,128)S(1)}, f32[4,8,1024]{2,1,0:T(8,128)S(1)}) custom-call(f32[40,1024]{1,0:T(8,128)S(1)} %get-tuple-element.23.own, f32[40,1024]{1,0:T(8,128)S(1)} %collective-permute-done.got), custom_call_target="tpu_custom_call" | custom-call | tf_op jit(solution)/shard_map/pallas_call | solution.py:363
  33.6 10.6 %shard_map.58 = (f32[24,1024]{1,0:T(8,128)S(1)}, bf16[72,256,768]{2,1,0:T(8,128)(2,1)S(1)}) custom-call(s32[3072]{0:T(1024)S(4)} %get-tuple-element.24.tab, f32[40,1024]{1,0:T(8,128)S(1)} %get-tuple-element.23.own, f32[40,1024]{1,0:T(8,128)S(1)} %collective-permute-done.got, ...), custom_call_target="tpu_custom_call", output_to_operand_aliasing={{1}: (6, {})} | custom-call | tf_op jit(solution)/shard_map/pallas_call | solution.py:373
  44.2 9.5 %shard_map.59 = (f32[24,1024]{1,0:T(8,128)S(1)}, bf16[72,256,768]{2,1,0:T(8,128)(2,1)S(1)}) custom-call(s32[3072]{0:T(1024)S(4)} %get-tuple-element.24.tab, f32[40,1024]{1,0:T(8,128)S(1)} %get-tuple-element.23.own, f32[40,1024]{1,0:T(8,128)S(1)} %collective-permute-done.got, ...), custom_call_target="tpu_custom_call", output_to_operand_aliasing={{1}: (6, {})} | custom-call | tf_op jit(solution)/shard_map/pallas_call | solution.py:373
  53.7 1.9 %collective-permute-start.3 = (f32[24,1024]{1,0:T(8,128)S(1)}, f32[24,1024]{1,0:T(8,128)S(1)}, u32[]{:S(2)}, u32[]{:S(2)}) collective-permute-start(f32[24,1024]{1,0:T(8,128)S(1)} %get-tuple-element.31), channel_id=1, source_target_pairs={{0,2},{2,0},{4,6},{6,4},{8,10},{10,8},{12,14},{14,12},{16,18},{18,... | collective-permute-start | bytes 294920 | tf_op jit(solution)/shard_map/ppermute | solution.py:349
  55.7 7.3 %collective-permute-start.4 = (f32[24,1024]{1,0:T(8,128)S(1)}, f32[24,1024]{1,0:T(8,128)S(1)}, u32[]{:S(2)}, u32[]{:S(2)}) collective-permute-start(f32[24,1024]{1,0:T(8,128)S(1)} %get-tuple-element.32), channel_id=1, source_target_pairs={{0,126},{2,4},{4,2},{6,8},{8,6},{10,12},{12,10},{14,16},{16,14},{1... | collective-permute-start | bytes 294920 | tf_op jit(solution)/shard_map/ppermute | solution.py:349
  62.9 2.0 %shard_map.60.field = f32[24,1024]{1,0:T(8,128)S(1)} custom-call(s32[3072]{0:T(1024)S(4)} %get-tuple-element.24.tab, f32[40,1024]{1,0:T(8,128)S(1)} %get-tuple-element.23.own, f32[40,1024]{1,0:T(8,128)S(1)} %collective-permute-done.got, f32[4,8,1024]{2,1,0:T(8,128)S(1)} %get-tuple-element.25.own_pos, f32[4,8,1024]{2,1,0:T(8,128)S(1)} %get-tuple-element.26.got_pos, ...), custom_call_target="tpu_custom_call" | custom-call | tf_op jit(solution)/shard_map/pallas_call | solution.py:383
  66.2 1.9 %collective-permute-start.5 = (f32[24,1024]{1,0:T(8,128)S(1)}, f32[24,1024]{1,0:T(8,128)S(1)}, u32[]{:S(2)}, u32[]{:S(2)}) collective-permute-start(f32[24,1024]{1,0:T(8,128)S(1)} %shard_map.61.own), channel_id=1, source_target_pairs={{0,1},{1,0},{2,3},{3,2},{4,5},{5,4},{6,7},{7,6},{8,9},{9,8},{10,11... | collective-permute-start | bytes 294920 | tf_op jit(solution)/shard_map/ppermute | solution.py:348
  68.1 3.2 %shard_map.63 = (f32[4,24,1024]{2,1,0:T(8,128)S(1)}, f32[4,24,1024]{2,1,0:T(8,128)S(1)}) custom-call(s32[3072]{0:T(1024)S(4)} %get-tuple-element.24.tab, f32[24,1024]{1,0:T(8,128)S(1)} %shard_map.61.own, f32[4,8,1024]{2,1,0:T(8,128)S(1)} %get-tuple-element.25.own_pos, f32[12,1024]{1,0:T(8,128)S(1)} %collective-permute-done.1.pos.pos_a, ...), custom_call_target="tpu_custom_call" | custom-call | tf_op jit(solution)/shard_map/pallas_call | solution.py:404
  73.0 7.3 %collective-permute-start.7 = (f32[24,1024]{1,0:T(8,128)S(1)}, f32[24,1024]{1,0:T(8,128)S(1)}, u32[]{:S(2)}, u32[]{:S(2)}) collective-permute-start(f32[24,1024]{1,0:T(8,128)S(1)} %shard_map.65), channel_id=1, source_target_pairs={{0,126},{2,4},{4,2},{6,8},{8,6},{10,12},{12,10},{14,16},{16,14},{1... | collective-permute-start | bytes 294920 | tf_op jit(solution)/shard_map/ppermute | solution.py:349
  83.2 2.2 %shard_map.62.field = f32[24,1024]{1,0:T(8,128)S(1)} custom-call(s32[3072]{0:T(1024)S(4)} %get-tuple-element.24.tab, f32[24,1024]{1,0:T(8,128)S(1)} %shard_map.61.own, f32[24,1024]{1,0:T(8,128)S(1)} %collective-permute-done.5.got, f32[4,8,1024]{2,1,0:T(8,128)S(1)} %get-tuple-element.25.own_pos, f32[4,8,1024]{2,1,0:T(8,128)S(1)} %get-tuple-element.26.got_pos, ...), custom_call_target="tpu_custom_call" | custom-call | tf_op jit(solution)/shard_map/pallas_call | solution.py:383
  85.4 2.4 %collective-permute-done.6.from_a = f32[24,1024]{1,0:T(8,128)S(1)} collective-permute-done((f32[24,1024]{1,0:T(8,128)S(1)}, f32[24,1024]{1,0:T(8,128)S(1)}, u32[]{:S(2)}, u32[]{:S(2)}) %collective-permute-start.6) | collective-permute-done | bytes 98336 | tf_op jit(solution)/shard_map/ppermute | solution.py:349
  89.7 3.2 %shard_map.68 = (f32[4,24,1024]{2,1,0:T(8,128)S(1)}, f32[4,24,1024]{2,1,0:T(8,128)S(1)}) custom-call(s32[3072]{0:T(1024)S(4)} %get-tuple-element.24.tab, f32[24,1024]{1,0:T(8,128)S(1)} %shard_map.66.own, f32[4,8,1024]{2,1,0:T(8,128)S(1)} %get-tuple-element.25.own_pos, f32[12,1024]{1,0:T(8,128)S(1)} %collective-permute-done.1.pos.pos_a, ...), custom_call_target="tpu_custom_call" | custom-call | tf_op jit(solution)/shard_map/pallas_call | solution.py:404
  94.6 3.6 %collective-permute-start.10 = (f32[24,1024]{1,0:T(8,128)S(1)}, f32[24,1024]{1,0:T(8,128)S(1)}, u32[]{:S(2)}, u32[]{:S(2)}) collective-permute-start(f32[24,1024]{1,0:T(8,128)S(1)} %shard_map.70), channel_id=1, source_target_pairs={{0,126},{2,4},{4,2},{6,8},{8,6},{10,12},{12,10},{14,16},{16,14},{1... | collective-permute-start | bytes 294920 | tf_op jit(solution)/shard_map/ppermute | solution.py:349
  99.1 1.9 %collective-permute-start.9 = (f32[24,1024]{1,0:T(8,128)S(1)}, f32[24,1024]{1,0:T(8,128)S(1)}, u32[]{:S(2)}, u32[]{:S(2)}) collective-permute-start(f32[24,1024]{1,0:T(8,128)S(1)} %shard_map.69), channel_id=1, source_target_pairs={{0,2},{2,0},{4,6},{6,4},{8,10},{10,8},{12,14},{14,12},{16,18},{18,... | collective-permute-start | bytes 294920 | tf_op jit(solution)/shard_map/ppermute | solution.py:349
  101.0 2.0 %shard_map.67.field = f32[24,1024]{1,0:T(8,128)S(1)} custom-call(s32[3072]{0:T(1024)S(4)} %get-tuple-element.24.tab, f32[24,1024]{1,0:T(8,128)S(1)} %shard_map.66.own, f32[24,1024]{1,0:T(8,128)S(1)} %collective-permute-done.8.got, f32[4,8,1024]{2,1,0:T(8,128)S(1)} %get-tuple-element.25.own_pos, f32[4,8,1024]{2,1,0:T(8,128)S(1)} %get-tuple-element.26.got_pos, ...), custom_call_target="tpu_custom_call" | custom-call | tf_op jit(solution)/shard_map/pallas_call | solution.py:383
  105.7 1.9 %collective-permute-start.11 = (f32[24,1024]{1,0:T(8,128)S(1)}, f32[24,1024]{1,0:T(8,128)S(1)}, u32[]{:S(2)}, u32[]{:S(2)}) collective-permute-start(f32[24,1024]{1,0:T(8,128)S(1)} %shard_map.71.own), channel_id=1, source_target_pairs={{0,1},{1,0},{2,3},{3,2},{4,5},{5,4},{6,7},{7,6},{8,9},{9,8},{10,11... | collective-permute-start | bytes 294920 | tf_op jit(solution)/shard_map/ppermute | solution.py:348
  107.6 3.2 %shard_map.73 = (f32[4,24,1024]{2,1,0:T(8,128)S(1)}, f32[4,24,1024]{2,1,0:T(8,128)S(1)}) custom-call(s32[3072]{0:T(1024)S(4)} %get-tuple-element.24.tab, f32[24,1024]{1,0:T(8,128)S(1)} %shard_map.71.own, f32[4,8,1024]{2,1,0:T(8,128)S(1)} %get-tuple-element.25.own_pos, f32[12,1024]{1,0:T(8,128)S(1)} %collective-permute-done.1.pos.pos_a, ...), custom_call_target="tpu_custom_call" | custom-call | tf_op jit(solution)/shard_map/pallas_call | solution.py:404
  112.5 7.2 %collective-permute-start.13 = (f32[24,1024]{1,0:T(8,128)S(1)}, f32[24,1024]{1,0:T(8,128)S(1)}, u32[]{:S(2)}, u32[]{:S(2)}) collective-permute-start(f32[24,1024]{1,0:T(8,128)S(1)} %shard_map.75), channel_id=1, source_target_pairs={{0,126},{2,4},{4,2},{6,8},{8,6},{10,12},{12,10},{14,16},{16,14},{1... | collective-permute-start | bytes 294920 | tf_op jit(solution)/shard_map/ppermute | solution.py:349
  122.5 2.0 %shard_map.72.field = f32[24,1024]{1,0:T(8,128)S(1)} custom-call(s32[3072]{0:T(1024)S(4)} %get-tuple-element.24.tab, f32[24,1024]{1,0:T(8,128)S(1)} %shard_map.71.own, f32[24,1024]{1,0:T(8,128)S(1)} %collective-permute-done.11.got, f32[4,8,1024]{2,1,0:T(8,128)S(1)} %get-tuple-element.25.own_pos, f32[4,8,1024]{2,1,0:T(8,128)S(1)} %get-tuple-element.26.got_pos, ...), custom_call_target="tpu_custom_call" | custom-call | tf_op jit(solution)/shard_map/pallas_call | solution.py:383
  124.6 2.5 %collective-permute-done.12.from_a = f32[24,1024]{1,0:T(8,128)S(1)} collective-permute-done((f32[24,1024]{1,0:T(8,128)S(1)}, f32[24,1024]{1,0:T(8,128)S(1)}, u32[]{:S(2)}, u32[]{:S(2)}) %collective-permute-start.12) | collective-permute-done | bytes 98336 | tf_op jit(solution)/shard_map/ppermute | solution.py:349
  127.2 8.4 %all_to_all.11 = f32[4,8,1024]{2,1,0:T(8,128)S(1)} all-to-all(f32[4,8,1024]{2,1,0:T(8,128)S(1)} %shard_map.76), channel_id=1, replica_groups=mesh['gx'=4,'gy'=64,'gz'=2] {'gx'}, dimensions={0} | all-to-all | bytes 262144 | tf_op jit(solution)/shard_map/all_to_all | solution.py:415
  (37 shorter events, 23.8 us)
Async XLA Ops:
  1.6 0.8 copy-start
  2.4 0.7 copy-start.1
  3.1 0.7 copy-start.2
  15.2 8.6 %collective-permute-start = (f32[40,1024]{1,0:T(8,128)S(1)}, f32[40,1024]{1,0:T(8,128)S(1)}, u32[]{:S(2)}, u32[]{:S(2)}) collective-permute-start(f32[40,1024]{1,0:T(8,128)S(1)} %get-tuple-element.23.own), channel_id=1, source_target_pairs={{0,1},{1,0},{2,3},{3,2},{4,5},{5,4},{6,7},{7,6},{8,9},{9,8},{10,11... | collective-permute-start | bytes 491528 | tf_op jit(solution)/shard_map/ppermute | solution.py:348
  17.1 16.4 %collective-permute-start.2 = (f32[12,1024]{1,0:T(8,128)S(1)}, f32[12,1024]{1,0:T(8,128)S(1)}, u32[]{:S(2)}, u32[]{:S(2)}) collective-permute-start(f32[12,1024]{1,0:T(8,128)S(1)} %get-tuple-element.27), channel_id=1, source_target_pairs={{0,126},{2,4},{4,2},{6,8},{8,6},{10,12},{12,10},{14,16},{16,14},{1... | collective-permute-start | bytes 147464 | tf_op jit(solution)/shard_map/ppermute | solution.py:349
  21.8 22.4 %collective-permute-start.1 = (f32[12,1024]{1,0:T(8,128)S(1)}, f32[12,1024]{1,0:T(8,128)S(1)}, u32[]{:S(2)}, u32[]{:S(2)}) collective-permute-start(f32[12,1024]{1,0:T(8,128)S(1)} %get-tuple-element.27), channel_id=1, source_target_pairs={{0,2},{2,0},{4,6},{6,4},{8,10},{10,8},{12,14},{14,12},{16,18},{18,... | collective-permute-start | bytes 147464 | tf_op jit(solution)/shard_map/ppermute | solution.py:349
  53.7 11.2 %collective-permute-start.3 = (f32[24,1024]{1,0:T(8,128)S(1)}, f32[24,1024]{1,0:T(8,128)S(1)}, u32[]{:S(2)}, u32[]{:S(2)}) collective-permute-start(f32[24,1024]{1,0:T(8,128)S(1)} %get-tuple-element.31), channel_id=1, source_target_pairs={{0,2},{2,0},{4,6},{6,4},{8,10},{10,8},{12,14},{14,12},{16,18},{18,... | collective-permute-start | bytes 294920 | tf_op jit(solution)/shard_map/ppermute | solution.py:349
  55.7 10.5 %collective-permute-start.4 = (f32[24,1024]{1,0:T(8,128)S(1)}, f32[24,1024]{1,0:T(8,128)S(1)}, u32[]{:S(2)}, u32[]{:S(2)}) collective-permute-start(f32[24,1024]{1,0:T(8,128)S(1)} %get-tuple-element.32), channel_id=1, source_target_pairs={{0,126},{2,4},{4,2},{6,8},{8,6},{10,12},{12,10},{14,16},{16,14},{1... | collective-permute-start | bytes 294920 | tf_op jit(solution)/shard_map/ppermute | solution.py:349
  66.2 5.1 %collective-permute-start.5 = (f32[24,1024]{1,0:T(8,128)S(1)}, f32[24,1024]{1,0:T(8,128)S(1)}, u32[]{:S(2)}, u32[]{:S(2)}) collective-permute-start(f32[24,1024]{1,0:T(8,128)S(1)} %shard_map.61.own), channel_id=1, source_target_pairs={{0,1},{1,0},{2,3},{3,2},{4,5},{5,4},{6,7},{7,6},{8,9},{9,8},{10,11... | collective-permute-start | bytes 294920 | tf_op jit(solution)/shard_map/ppermute | solution.py:348
  73.0 12.4 %collective-permute-start.7 = (f32[24,1024]{1,0:T(8,128)S(1)}, f32[24,1024]{1,0:T(8,128)S(1)}, u32[]{:S(2)}, u32[]{:S(2)}) collective-permute-start(f32[24,1024]{1,0:T(8,128)S(1)} %shard_map.65), channel_id=1, source_target_pairs={{0,126},{2,4},{4,2},{6,8},{8,6},{10,12},{12,10},{14,16},{16,14},{1... | collective-permute-start | bytes 294920 | tf_op jit(solution)/shard_map/ppermute | solution.py:349
  81.2 6.5 %collective-permute-start.6 = (f32[24,1024]{1,0:T(8,128)S(1)}, f32[24,1024]{1,0:T(8,128)S(1)}, u32[]{:S(2)}, u32[]{:S(2)}) collective-permute-start(f32[24,1024]{1,0:T(8,128)S(1)} %shard_map.64), channel_id=1, source_target_pairs={{0,2},{2,0},{4,6},{6,4},{8,10},{10,8},{12,14},{14,12},{16,18},{18,... | collective-permute-start | bytes 294920 | tf_op jit(solution)/shard_map/ppermute | solution.py:349
  87.8 5.1 %collective-permute-start.8 = (f32[24,1024]{1,0:T(8,128)S(1)}, f32[24,1024]{1,0:T(8,128)S(1)}, u32[]{:S(2)}, u32[]{:S(2)}) collective-permute-start(f32[24,1024]{1,0:T(8,128)S(1)} %shard_map.66.own), channel_id=1, source_target_pairs={{0,1},{1,0},{2,3},{3,2},{4,5},{5,4},{6,7},{7,6},{8,9},{9,8},{10,11... | collective-permute-start | bytes 294920 | tf_op jit(solution)/shard_map/ppermute | solution.py:348
  94.6 9.8 %collective-permute-start.10 = (f32[24,1024]{1,0:T(8,128)S(1)}, f32[24,1024]{1,0:T(8,128)S(1)}, u32[]{:S(2)}, u32[]{:S(2)}) collective-permute-start(f32[24,1024]{1,0:T(8,128)S(1)} %shard_map.70), channel_id=1, source_target_pairs={{0,126},{2,4},{4,2},{6,8},{8,6},{10,12},{12,10},{14,16},{16,14},{1... | collective-permute-start | bytes 294920 | tf_op jit(solution)/shard_map/ppermute | solution.py:349
  99.1 6.5 %collective-permute-start.9 = (f32[24,1024]{1,0:T(8,128)S(1)}, f32[24,1024]{1,0:T(8,128)S(1)}, u32[]{:S(2)}, u32[]{:S(2)}) collective-permute-start(f32[24,1024]{1,0:T(8,128)S(1)} %shard_map.69), channel_id=1, source_target_pairs={{0,2},{2,0},{4,6},{6,4},{8,10},{10,8},{12,14},{14,12},{16,18},{18,... | collective-permute-start | bytes 294920 | tf_op jit(solution)/shard_map/ppermute | solution.py:349
  105.7 5.1 %collective-permute-start.11 = (f32[24,1024]{1,0:T(8,128)S(1)}, f32[24,1024]{1,0:T(8,128)S(1)}, u32[]{:S(2)}, u32[]{:S(2)}) collective-permute-start(f32[24,1024]{1,0:T(8,128)S(1)} %shard_map.71.own), channel_id=1, source_target_pairs={{0,1},{1,0},{2,3},{3,2},{4,5},{5,4},{6,7},{7,6},{8,9},{9,8},{10,11... | collective-permute-start | bytes 294920 | tf_op jit(solution)/shard_map/ppermute | solution.py:348
  112.5 12.1 %collective-permute-start.13 = (f32[24,1024]{1,0:T(8,128)S(1)}, f32[24,1024]{1,0:T(8,128)S(1)}, u32[]{:S(2)}, u32[]{:S(2)}) collective-permute-start(f32[24,1024]{1,0:T(8,128)S(1)} %shard_map.75), channel_id=1, source_target_pairs={{0,126},{2,4},{4,2},{6,8},{8,6},{10,12},{12,10},{14,16},{16,14},{1... | collective-permute-start | bytes 294920 | tf_op jit(solution)/shard_map/ppermute | solution.py:349
  120.6 6.5 %collective-permute-start.12 = (f32[24,1024]{1,0:T(8,128)S(1)}, f32[24,1024]{1,0:T(8,128)S(1)}, u32[]{:S(2)}, u32[]{:S(2)}) collective-permute-start(f32[24,1024]{1,0:T(8,128)S(1)} %shard_map.74), channel_id=1, source_target_pairs={{0,2},{2,0},{4,6},{6,4},{8,10},{10,8},{12,14},{14,12},{16,18},{18,... | collective-permute-start | bytes 294920 | tf_op jit(solution)/shard_map/ppermute | solution.py:349

commit v4 on v3

--- a/solution.py
+++ b/solution.py
@@ -234,7 +234,6 @@
         copy.wait()
     sort_entries(lists, tab)
     each_build(tab, 0, own_pos, own_pos, tens)
-    each_build(tab, 3, got_pos, own_pos, tens)
 
 
 def first_far_kernel(slot, tab, own, got, own_pos, got_pos, pos, tens_in, out, tens, tgt_pos, acc, one):
@@ -271,6 +270,11 @@
     settle(acc, out)
 
 
+def first_here_kernel(tab, own, got, own_pos, got_pos, tens_in, out, tens, acc, one):
+    each_build(tab, 3, got_pos, own_pos, tens)
+    here_kernel(tab, own, got, own_pos, got_pos, tens, out, acc, one)
+
+
 def respond_rows(alpha, total):
     real_row = lax.broadcasted_iota(jnp.int32, (8, total.shape[1]), 0) % 2 < 1
     turned = jnp.where(real_row, pltpu.roll(total, 7, 0), pltpu.roll(total, 1, 0))
@@ -285,24 +289,28 @@
 
 
 def last_kernel(field, from_a, from_b, applied, alpha, out):
-    out[...] = jnp.zeros_like(out)
     for a in range(3):
         rows = slice(8 * a, 8 * a + 8)
         total = applied[rows, :] + coupling * (field[rows, :] + from_a[rows, :] + from_b[rows, :])
         dip = respond_rows(alpha[...], total)
         for s in range(SLABS):
-            for i in range(2):
-                out[s, 3 * i + a : 3 * i + a + 1, :] = dip[2 * s + i : 2 * s + i + 1]
-
-
-def pack_kernel(pos, pol, field, codes, count, out):
+            out[s, a] = dip[2 * s : 2 * s + 2]
+
+
+def pack_kernel(pos_in, pol_in, field_in, codes_in, count, out, pos, pol, field, codes, sems):
+    pairs = ((field_in, field), (pol_in, pol), (pos_in, pos), (codes_in, codes))
+    copies = [pltpu.make_async_copy(a, b, sems.at[k]) for k, (a, b) in enumerate(pairs)]
+    for copy in copies:
+        copy.start()
+    for copy in copies:
+        copy.wait()
     lane = lax.broadcasted_iota(jnp.int32, (1, BLOCK), 1)
     row = jnp.where(lane == codes.shape[0], count[0], 0)
     for p in range(codes.shape[0]):
         row = jnp.where(lane == p, codes[p], row)
     for f in range(SLABS):
-        for i in range(2):
-            out[f, 3 * i : 3 * i + 3, :] = field[f, i]
+        for a in range(3):
+            out[f, 2 * a : 2 * a + 2, :] = field[f, a]
         out[f, 6:8, :] = pol[f]
         out[f, 8:16, :] = jnp.zeros((8, out.shape[2]), jnp.float32)
         out[f, 8:11, :] = pos[...]
@@ -311,10 +319,10 @@
 
 def join_kernel(got, applied, alpha, own, pos):
     for s in range(SLABS):
-        for i in range(2):
-            for a in range(3):
+        for a in range(3):
+            for i in range(2):
                 row = 8 * a + 2 * s + i
-                applied[row : row + 1, :] = got[s, 3 * i + a : 3 * i + a + 1, :]
+                applied[row : row + 1, :] = got[s, 2 * a + i : 2 * a + i + 1, :]
         real, imag = got[s, 6:7, :], got[s, 7:8, :]
         alpha[2 * s : 2 * s + 1, :] = real
         alpha[2 * s + 1 : 2 * s + 2, :] = real
@@ -349,9 +357,20 @@
     turn = lambda value, first: lax.ppermute(value, "gy", swaps(lax.axis_size("gy"), first))
     keep = lambda value: pltpu.with_memory_space_constraint(value, pltpu.VMEM)
     fixed = lambda value: pltpu.with_memory_space_constraint(value, pltpu.SMEM)
-    sent = call(pack_kernel, arr(SLABS, 16), (), [VMEM] * 3 + [SMEM] * 2, VMEM)(
-        positions, polarizability, applied_field, pair_codes, pair_counts
+    arguments = (
+        positions,
+        polarizability,
+        jnp.transpose(applied_field, (0, 2, 1, 3)),
+        pair_codes,
     )
+    sent = call(
+        pack_kernel,
+        arr(SLABS, 16),
+        [pltpu.VMEM(value.shape, f32) for value in arguments[:3]]
+        + [pltpu.SMEM(pair_codes.shape, jnp.int32), pltpu.SemaphoreType.DMA((4,))],
+        [pl.BlockSpec(memory_space=pltpu.HBM)] * 4 + [SMEM],
+        VMEM,
+    )(*[pltpu.with_memory_space_constraint(value, pltpu.HBM) for value in arguments], pair_counts)
     got = lax.all_to_all(sent, "gx", 0, 0)
     applied, alpha, own, pos = call(join_kernel, (arr(24), arr(16), arr(40), arr(12)))(got)
     got = flip(own)
@@ -397,7 +416,14 @@
     from_b = turn(msg, False)
     msg, tens = first_far(1, pos_a, tens)
     from_a = turn(msg, True)
-    field = here(own, got)
+    field, tens = call(
+        first_here_kernel,
+        (arr(24), tens_shape),
+        (acc, one),
+        [SMEM] + [VMEM] * 5,
+        (VMEM, VMEM),
+        {5: 1},
+    )(tab, own, got, own_pos, got_pos, keep(tens))
     for sweep in range(1, ITERS):
         own = call(update_kernel, arr(24))(field, from_a, from_b, applied, alpha)
         got = flip(own)
@@ -411,9 +437,8 @@
         from_b = turn(far(2, got, pos_b, at_b), False)
         from_a = turn(far(1, got, pos_a, at_a), True)
         field = here(own, got)
-    out = call(last_kernel, arr(SLABS, 8))(field, from_a, from_b, applied, alpha)
-    out = lax.all_to_all(out, "gx", 0, 0)
-    return out[:, :6].reshape(SLABS, 2, 3, rows)
+    out = call(last_kernel, arr(SLABS, 3, 2))(field, from_a, from_b, applied, alpha)
+    return jnp.transpose(lax.all_to_all(out, "gx", 0, 0), (0, 2, 1, 3))
 
 
 def solution(mesh):

time: 137 us -> 116 us (0.85)
  the two profiles are of different devices: /device:TPU:248 before, /device:TPU:1 now
where the time goes in v4:
time: 116 us; the launch traced here: 114 us
  starting transfers between devices  67.3 us (58%)
  Pallas kernels  20.7 us (18%)
  blocking collectives  17.2 us (15%)
  waiting for transfers between devices  7.3 us (6%)
    ppermute x10, starting transfers between devices, shards(): lax.ppermute(value, 'gy', swaps(lax.axis_size('gy'), first))  48.3 us
    ppermute x4, starting transfers between devices, shards(): flip = lambda value: lax.ppermute(value, 'gz', swaps(2, True))  19 us
    all_to_all x1, blocking collectives, shards(): got = lax.all_to_all(sent, 'gx', 0, 0)  10.2 us
    ppermute x10, waiting for transfers between devices, shards(): lax.ppermute(value, 'gy', swaps(lax.axis_size('gy'), first))  7.16 us
    all_to_all x1, blocking collectives, shards(): return jnp.transpose(lax.all_to_all(out, 'gx', 0, 0), (0, 2, 1, 3))  7.03 us
    pallas_call x2, Pallas kernels, first_far(): call(functools.partial(first_far_kernel, slot), (arr(24), tens_shape), (t...  4.59 us
    pallas_call x3, Pallas kernels, here(): call(here_kernel, arr(24), (acc, one), [SMEM] + [VMEM] * 5, VMEM)  3.92 us
    pallas_call x6, Pallas kernels, far(): call(functools.partial(far_kernel, slot), arr(24), (tgt_pos, acc, one), [...  2.99 us
  transfers between devices with their start and end apart: 14, of which 3 were waited for; matrix products, arithmetic and copies ran while one was open for 0% of the time, Pallas kernels for 14%

profile of v4, /device:TPU:1, one launch (start us, length us, event | category | flops | bytes accessed | tf_op | source)
XLA Modules:
  0.0 114.1 jit_solution(9417733126043608402)
XLA Ops:
  1.7 10.2 %all_to_all.10.got = f32[4,16,1024]{2,1,0:T(8,128)S(1)} all-to-all(f32[4,16,1024]{2,1,0:T(8,128)S(1)} %shard_map.55), channel_id=1, replica_groups=mesh['gx'=4,'gy'=64,'gz'=2] {'gx'}, dimensions={0} | all-to-all | bytes 524288 | tf_op jit(solution)/shard_map/all_to_all | solution.py:374
  11.9 7.7 %collective-permute-start = (f32[40,1024]{1,0:T(8,128)S(1)}, f32[40,1024]{1,0:T(8,128)S(1)}, u32[]{:S(2)}, u32[]{:S(2)}) collective-permute-start(f32[40,1024]{1,0:T(8,128)S(1)} %get-tuple-element.25.own), channel_id=1, source_target_pairs={{0,1},{1,0},{2,3},{3,2},{4,5},{5,4},{6,7},{7,6},{8,9},{9,8},{10,11... | collective-permute-start | bytes 491528 | tf_op jit(solution)/shard_map/ppermute | solution.py:356
  19.6 9.9 %collective-permute-start.2 = (f32[12,1024]{1,0:T(8,128)S(1)}, f32[12,1024]{1,0:T(8,128)S(1)}, u32[]{:S(2)}, u32[]{:S(2)}) collective-permute-start(f32[12,1024]{1,0:T(8,128)S(1)} %get-tuple-element.29), channel_id=1, source_target_pairs={{0,126},{2,4},{4,2},{6,8},{8,6},{10,12},{12,10},{14,16},{16,14},{1... | collective-permute-start | bytes 147464 | tf_op jit(solution)/shard_map/ppermute | solution.py:357
  29.5 1.9 %collective-permute-start.1 = (f32[12,1024]{1,0:T(8,128)S(1)}, f32[12,1024]{1,0:T(8,128)S(1)}, u32[]{:S(2)}, u32[]{:S(2)}) collective-permute-start(f32[12,1024]{1,0:T(8,128)S(1)} %get-tuple-element.29), channel_id=1, source_target_pairs={{0,2},{2,0},{4,6},{6,4},{8,10},{10,8},{12,14},{14,12},{16,18},{18,... | collective-permute-start | bytes 147464 | tf_op jit(solution)/shard_map/ppermute | solution.py:357
  31.5 2.4 %shard_map.57 = (bf16[72,256,768]{2,1,0:T(8,128)(2,1)S(1)}, s32[3072]{0:T(1024)S(4)}, f32[4,8,1024]{2,1,0:T(8,128)S(1)}, f32[4,8,1024]{2,1,0:T(8,128)S(1)}) custom-call(f32[40,1024]{1,0:T(8,128)S(1)} %get-tuple-element.25.own, f32[40,1024]{1,0:T(8,128)S(1)} %collective-permute-done.got), custom_call_target="tpu_custom_call" | custom-call | tf_op jit(solution)/shard_map/pallas_call | solution.py:382
  33.8 2.6 %shard_map.58 = (f32[24,1024]{1,0:T(8,128)S(1)}, bf16[72,256,768]{2,1,0:T(8,128)(2,1)S(1)}) custom-call(s32[3072]{0:T(1024)S(4)} %get-tuple-element.26.tab, f32[40,1024]{1,0:T(8,128)S(1)} %get-tuple-element.25.own, f32[40,1024]{1,0:T(8,128)S(1)} %collective-permute-done.got, ...), custom_call_target="tpu_custom_call", output_to_operand_aliasing={{1}: (6, {})} | custom-call | tf_op jit(solution)/shard_map/pallas_call | solution.py:392
  36.4 2.0 %shard_map.59 = (f32[24,1024]{1,0:T(8,128)S(1)}, bf16[72,256,768]{2,1,0:T(8,128)(2,1)S(1)}) custom-call(s32[3072]{0:T(1024)S(4)} %get-tuple-element.26.tab, f32[40,1024]{1,0:T(8,128)S(1)} %get-tuple-element.25.own, f32[40,1024]{1,0:T(8,128)S(1)} %collective-permute-done.got, ...), custom_call_target="tpu_custom_call", output_to_operand_aliasing={{1}: (6, {})} | custom-call | tf_op jit(solution)/shard_map/pallas_call | solution.py:392
  38.5 6.7 %collective-permute-start.3 = (f32[24,1024]{1,0:T(8,128)S(1)}, f32[24,1024]{1,0:T(8,128)S(1)}, u32[]{:S(2)}, u32[]{:S(2)}) collective-permute-start(f32[24,1024]{1,0:T(8,128)S(1)} %get-tuple-element.34), channel_id=1, source_target_pairs={{0,2},{2,0},{4,6},{6,4},{8,10},{10,8},{12,14},{14,12},{16,18},{18,... | collective-permute-start | bytes 294920 | tf_op jit(solution)/shard_map/ppermute | solution.py:357
  45.2 9.6 %collective-permute-start.4 = (f32[24,1024]{1,0:T(8,128)S(1)}, f32[24,1024]{1,0:T(8,128)S(1)}, u32[]{:S(2)}, u32[]{:S(2)}) collective-permute-start(f32[24,1024]{1,0:T(8,128)S(1)} %get-tuple-element.35), channel_id=1, source_target_pairs={{0,126},{2,4},{4,2},{6,8},{8,6},{10,12},{12,10},{14,16},{16,14},{1... | collective-permute-start | bytes 294920 | tf_op jit(solution)/shard_map/ppermute | solution.py:357
  54.8 2.9 %shard_map.60 = (f32[24,1024]{1,0:T(8,128)S(1)}, bf16[72,256,768]{2,1,0:T(8,128)(2,1)S(1)}) custom-call(s32[3072]{0:T(1024)S(4)} %get-tuple-element.26.tab, f32[40,1024]{1,0:T(8,128)S(1)} %get-tuple-element.25.own, f32[40,1024]{1,0:T(8,128)S(1)} %collective-permute-done.got, ...), custom_call_target="tpu_custom_call", output_to_operand_aliasing={{1}: (5, {})} | custom-call | tf_op jit(solution)/shard_map/pallas_call | solution.py:419
  57.9 2.7 %collective-permute-start.5 = (f32[24,1024]{1,0:T(8,128)S(1)}, f32[24,1024]{1,0:T(8,128)S(1)}, u32[]{:S(2)}, u32[]{:S(2)}) collective-permute-start(f32[24,1024]{1,0:T(8,128)S(1)} %shard_map.61.own), channel_id=1, source_target_pairs={{0,1},{1,0},{2,3},{3,2},{4,5},{5,4},{6,7},{7,6},{8,9},{9,8},{10,11... | collective-permute-start | bytes 294920 | tf_op jit(solution)/shard_map/ppermute | solution.py:356
  62.0 6.3 %collective-permute-start.7 = (f32[24,1024]{1,0:T(8,128)S(1)}, f32[24,1024]{1,0:T(8,128)S(1)}, u32[]{:S(2)}, u32[]{:S(2)}) collective-permute-start(f32[24,1024]{1,0:T(8,128)S(1)} %shard_map.65), channel_id=1, source_target_pairs={{0,126},{2,4},{4,2},{6,8},{8,6},{10,12},{12,10},{14,16},{16,14},{1... | collective-permute-start | bytes 294920 | tf_op jit(solution)/shard_map/ppermute | solution.py:357
  68.8 1.9 %collective-permute-start.6 = (f32[24,1024]{1,0:T(8,128)S(1)}, f32[24,1024]{1,0:T(8,128)S(1)}, u32[]{:S(2)}, u32[]{:S(2)}) collective-permute-start(f32[24,1024]{1,0:T(8,128)S(1)} %shard_map.64), channel_id=1, source_target_pairs={{0,2},{2,0},{4,6},{6,4},{8,10},{10,8},{12,14},{14,12},{16,18},{18,... | collective-permute-start | bytes 294920 | tf_op jit(solution)/shard_map/ppermute | solution.py:357
  70.7 1.4 %shard_map.62.field = f32[24,1024]{1,0:T(8,128)S(1)} custom-call(s32[3072]{0:T(1024)S(4)} %get-tuple-element.26.tab, f32[24,1024]{1,0:T(8,128)S(1)} %shard_map.61.own, f32[24,1024]{1,0:T(8,128)S(1)} %collective-permute-done.5.got, f32[4,8,1024]{2,1,0:T(8,128)S(1)} %get-tuple-element.27.own_pos, f32[4,8,1024]{2,1,0:T(8,128)S(1)} %get-tuple-element.28.got_pos, ...), custom_call_target="tpu_custom_call" | custom-call | tf_op jit(solution)/shard_map/pallas_call | solution.py:402
  72.1 2.0 %collective-permute-done.6.from_a = f32[24,1024]{1,0:T(8,128)S(1)} collective-permute-done((f32[24,1024]{1,0:T(8,128)S(1)}, f32[24,1024]{1,0:T(8,128)S(1)}, u32[]{:S(2)}, u32[]{:S(2)}) %collective-permute-start.6) | collective-permute-done | bytes 98336 | tf_op jit(solution)/shard_map/ppermute | solution.py:357
  74.2 4.9 %collective-permute-start.8 = (f32[24,1024]{1,0:T(8,128)S(1)}, f32[24,1024]{1,0:T(8,128)S(1)}, u32[]{:S(2)}, u32[]{:S(2)}) collective-permute-start(f32[24,1024]{1,0:T(8,128)S(1)} %shard_map.66.own), channel_id=1, source_target_pairs={{0,1},{1,0},{2,3},{3,2},{4,5},{5,4},{6,7},{7,6},{8,9},{9,8},{10,11... | collective-permute-start | bytes 294920 | tf_op jit(solution)/shard_map/ppermute | solution.py:356
  80.5 1.9 %collective-permute-start.10 = (f32[24,1024]{1,0:T(8,128)S(1)}, f32[24,1024]{1,0:T(8,128)S(1)}, u32[]{:S(2)}, u32[]{:S(2)}) collective-permute-start(f32[24,1024]{1,0:T(8,128)S(1)} %shard_map.70), channel_id=1, source_target_pairs={{0,126},{2,4},{4,2},{6,8},{8,6},{10,12},{12,10},{14,16},{16,14},{1... | collective-permute-start | bytes 294920 | tf_op jit(solution)/shard_map/ppermute | solution.py:357
  82.9 2.0 %collective-permute-start.9 = (f32[24,1024]{1,0:T(8,128)S(1)}, f32[24,1024]{1,0:T(8,128)S(1)}, u32[]{:S(2)}, u32[]{:S(2)}) collective-permute-start(f32[24,1024]{1,0:T(8,128)S(1)} %shard_map.69), channel_id=1, source_target_pairs={{0,2},{2,0},{4,6},{6,4},{8,10},{10,8},{12,14},{14,12},{16,18},{18,... | collective-permute-start | bytes 294920 | tf_op jit(solution)/shard_map/ppermute | solution.py:357
  86.2 3.0 %collective-permute-done.10.from_b = f32[24,1024]{1,0:T(8,128)S(1)} collective-permute-done((f32[24,1024]{1,0:T(8,128)S(1)}, f32[24,1024]{1,0:T(8,128)S(1)}, u32[]{:S(2)}, u32[]{:S(2)}) %collective-permute-start.10) | collective-permute-done | bytes 98336 | tf_op jit(solution)/shard_map/ppermute | solution.py:357
  89.2 3.8 %collective-permute-start.11 = (f32[24,1024]{1,0:T(8,128)S(1)}, f32[24,1024]{1,0:T(8,128)S(1)}, u32[]{:S(2)}, u32[]{:S(2)}) collective-permute-start(f32[24,1024]{1,0:T(8,128)S(1)} %shard_map.71.own), channel_id=1, source_target_pairs={{0,1},{1,0},{2,3},{3,2},{4,5},{5,4},{6,7},{7,6},{8,9},{9,8},{10,11... | collective-permute-start | bytes 294920 | tf_op jit(solution)/shard_map/ppermute | solution.py:356
  94.4 6.1 %collective-permute-start.13 = (f32[24,1024]{1,0:T(8,128)S(1)}, f32[24,1024]{1,0:T(8,128)S(1)}, u32[]{:S(2)}, u32[]{:S(2)}) collective-permute-start(f32[24,1024]{1,0:T(8,128)S(1)} %shard_map.75), channel_id=1, source_target_pairs={{0,126},{2,4},{4,2},{6,8},{8,6},{10,12},{12,10},{14,16},{16,14},{1... | collective-permute-start | bytes 294920 | tf_op jit(solution)/shard_map/ppermute | solution.py:357
  101.0 1.9 %collective-permute-start.12 = (f32[24,1024]{1,0:T(8,128)S(1)}, f32[24,1024]{1,0:T(8,128)S(1)}, u32[]{:S(2)}, u32[]{:S(2)}) collective-permute-start(f32[24,1024]{1,0:T(8,128)S(1)} %shard_map.74), channel_id=1, source_target_pairs={{0,2},{2,0},{4,6},{6,4},{8,10},{10,8},{12,14},{14,12},{16,18},{18,... | collective-permute-start | bytes 294920 | tf_op jit(solution)/shard_map/ppermute | solution.py:357
  104.2 2.2 %collective-permute-done.12.from_a = f32[24,1024]{1,0:T(8,128)S(1)} collective-permute-done((f32[24,1024]{1,0:T(8,128)S(1)}, f32[24,1024]{1,0:T(8,128)S(1)}, u32[]{:S(2)}, u32[]{:S(2)}) %collective-permute-start.12) | collective-permute-done | bytes 98336 | tf_op jit(solution)/shard_map/ppermute | solution.py:357
  106.4 7.0 %all_to_all.11 = f32[4,3,2,1024]{3,2,1,0:T(2,128)S(1)} all-to-all(f32[4,3,2,1024]{3,2,1,0:T(2,128)S(1)} %shard_map.76), channel_id=1, replica_groups=mesh['gx'=4,'gy'=64,'gz'=2] {'gx'}, dimensions={0} | all-to-all | bytes 196608 | tf_op jit(solution)/shard_map/all_to_all | solution.py:441
  (29 shorter events, 10.2 us)
Async XLA Ops:
  11.9 19.5 %collective-permute-start = (f32[40,1024]{1,0:T(8,128)S(1)}, f32[40,1024]{1,0:T(8,128)S(1)}, u32[]{:S(2)}, u32[]{:S(2)}) collective-permute-start(f32[40,1024]{1,0:T(8,128)S(1)} %get-tuple-element.25.own), channel_id=1, source_target_pairs={{0,1},{1,0},{2,3},{3,2},{4,5},{5,4},{6,7},{7,6},{8,9},{9,8},{10,11... | collective-permute-start | bytes 491528 | tf_op jit(solution)/shard_map/ppermute | solution.py:356
  19.6 14.2 %collective-permute-start.2 = (f32[12,1024]{1,0:T(8,128)S(1)}, f32[12,1024]{1,0:T(8,128)S(1)}, u32[]{:S(2)}, u32[]{:S(2)}) collective-permute-start(f32[12,1024]{1,0:T(8,128)S(1)} %get-tuple-element.29), channel_id=1, source_target_pairs={{0,126},{2,4},{4,2},{6,8},{8,6},{10,12},{12,10},{14,16},{16,14},{1... | collective-permute-start | bytes 147464 | tf_op jit(solution)/shard_map/ppermute | solution.py:357
  29.5 6.9 %collective-permute-start.1 = (f32[12,1024]{1,0:T(8,128)S(1)}, f32[12,1024]{1,0:T(8,128)S(1)}, u32[]{:S(2)}, u32[]{:S(2)}) collective-permute-start(f32[12,1024]{1,0:T(8,128)S(1)} %get-tuple-element.29), channel_id=1, source_target_pairs={{0,2},{2,0},{4,6},{6,4},{8,10},{10,8},{12,14},{14,12},{16,18},{18,... | collective-permute-start | bytes 147464 | tf_op jit(solution)/shard_map/ppermute | solution.py:357
  38.5 19.3 %collective-permute-start.3 = (f32[24,1024]{1,0:T(8,128)S(1)}, f32[24,1024]{1,0:T(8,128)S(1)}, u32[]{:S(2)}, u32[]{:S(2)}) collective-permute-start(f32[24,1024]{1,0:T(8,128)S(1)} %get-tuple-element.34), channel_id=1, source_target_pairs={{0,2},{2,0},{4,6},{6,4},{8,10},{10,8},{12,14},{14,12},{16,18},{18,... | collective-permute-start | bytes 294920 | tf_op jit(solution)/shard_map/ppermute | solution.py:357
  45.2 12.6 %collective-permute-start.4 = (f32[24,1024]{1,0:T(8,128)S(1)}, f32[24,1024]{1,0:T(8,128)S(1)}, u32[]{:S(2)}, u32[]{:S(2)}) collective-permute-start(f32[24,1024]{1,0:T(8,128)S(1)} %get-tuple-element.35), channel_id=1, source_target_pairs={{0,126},{2,4},{4,2},{6,8},{8,6},{10,12},{12,10},{14,16},{16,14},{1... | collective-permute-start | bytes 294920 | tf_op jit(solution)/shard_map/ppermute | solution.py:357
  57.9 3.6 %collective-permute-start.5 = (f32[24,1024]{1,0:T(8,128)S(1)}, f32[24,1024]{1,0:T(8,128)S(1)}, u32[]{:S(2)}, u32[]{:S(2)}) collective-permute-start(f32[24,1024]{1,0:T(8,128)S(1)} %shard_map.61.own), channel_id=1, source_target_pairs={{0,1},{1,0},{2,3},{3,2},{4,5},{5,4},{6,7},{7,6},{8,9},{9,8},{10,11... | collective-permute-start | bytes 294920 | tf_op jit(solution)/shard_map/ppermute | solution.py:356
  62.0 10.2 %collective-permute-start.7 = (f32[24,1024]{1,0:T(8,128)S(1)}, f32[24,1024]{1,0:T(8,128)S(1)}, u32[]{:S(2)}, u32[]{:S(2)}) collective-permute-start(f32[24,1024]{1,0:T(8,128)S(1)} %shard_map.65), channel_id=1, source_target_pairs={{0,126},{2,4},{4,2},{6,8},{8,6},{10,12},{12,10},{14,16},{16,14},{1... | collective-permute-start | bytes 294920 | tf_op jit(solution)/shard_map/ppermute | solution.py:357
  68.8 5.4 %collective-permute-start.6 = (f32[24,1024]{1,0:T(8,128)S(1)}, f32[24,1024]{1,0:T(8,128)S(1)}, u32[]{:S(2)}, u32[]{:S(2)}) collective-permute-start(f32[24,1024]{1,0:T(8,128)S(1)} %shard_map.64), channel_id=1, source_target_pairs={{0,2},{2,0},{4,6},{6,4},{8,10},{10,8},{12,14},{14,12},{16,18},{18,... | collective-permute-start | bytes 294920 | tf_op jit(solution)/shard_map/ppermute | solution.py:357
  74.2 5.8 %collective-permute-start.8 = (f32[24,1024]{1,0:T(8,128)S(1)}, f32[24,1024]{1,0:T(8,128)S(1)}, u32[]{:S(2)}, u32[]{:S(2)}) collective-permute-start(f32[24,1024]{1,0:T(8,128)S(1)} %shard_map.66.own), channel_id=1, source_target_pairs={{0,1},{1,0},{2,3},{3,2},{4,5},{5,4},{6,7},{7,6},{8,9},{9,8},{10,11... | collective-permute-start | bytes 294920 | tf_op jit(solution)/shard_map/ppermute | solution.py:356
  80.5 8.7 %collective-permute-start.10 = (f32[24,1024]{1,0:T(8,128)S(1)}, f32[24,1024]{1,0:T(8,128)S(1)}, u32[]{:S(2)}, u32[]{:S(2)}) collective-permute-start(f32[24,1024]{1,0:T(8,128)S(1)} %shard_map.70), channel_id=1, source_target_pairs={{0,126},{2,4},{4,2},{6,8},{8,6},{10,12},{12,10},{14,16},{16,14},{1... | collective-permute-start | bytes 294920 | tf_op jit(solution)/shard_map/ppermute | solution.py:357
  82.9 6.2 %collective-permute-start.9 = (f32[24,1024]{1,0:T(8,128)S(1)}, f32[24,1024]{1,0:T(8,128)S(1)}, u32[]{:S(2)}, u32[]{:S(2)}) collective-permute-start(f32[24,1024]{1,0:T(8,128)S(1)} %shard_map.69), channel_id=1, source_target_pairs={{0,2},{2,0},{4,6},{6,4},{8,10},{10,8},{12,14},{14,12},{16,18},{18,... | collective-permute-start | bytes 294920 | tf_op jit(solution)/shard_map/ppermute | solution.py:357
  89.2 4.7 %collective-permute-start.11 = (f32[24,1024]{1,0:T(8,128)S(1)}, f32[24,1024]{1,0:T(8,128)S(1)}, u32[]{:S(2)}, u32[]{:S(2)}) collective-permute-start(f32[24,1024]{1,0:T(8,128)S(1)} %shard_map.71.own), channel_id=1, source_target_pairs={{0,1},{1,0},{2,3},{3,2},{4,5},{5,4},{6,7},{7,6},{8,9},{9,8},{10,11... | collective-permute-start | bytes 294920 | tf_op jit(solution)/shard_map/ppermute | solution.py:356
  94.4 9.8 %collective-permute-start.13 = (f32[24,1024]{1,0:T(8,128)S(1)}, f32[24,1024]{1,0:T(8,128)S(1)}, u32[]{:S(2)}, u32[]{:S(2)}) collective-permute-start(f32[24,1024]{1,0:T(8,128)S(1)} %shard_map.75), channel_id=1, source_target_pairs={{0,126},{2,4},{4,2},{6,8},{8,6},{10,12},{12,10},{14,16},{16,14},{1... | collective-permute-start | bytes 294920 | tf_op jit(solution)/shard_map/ppermute | solution.py:357
  101.0 5.4 %collective-permute-start.12 = (f32[24,1024]{1,0:T(8,128)S(1)}, f32[24,1024]{1,0:T(8,128)S(1)}, u32[]{:S(2)}, u32[]{:S(2)}) collective-permute-start(f32[24,1024]{1,0:T(8,128)S(1)} %shard_map.74), channel_id=1, source_target_pairs={{0,2},{2,0},{4,6},{6,4},{8,10},{10,8},{12,14},{14,12},{16,18},{18,... | collective-permute-start | bytes 294920 | tf_op jit(solution)/shard_map/ppermute | solution.py:357
